TPU v7x, 32 devices: a whole 2x2x4 slice. The times are simulated.
32 devices in a mesh: row: 16 (over z, y, core), col: 2 (over x).
Axes of the slice: x: 2, y: 2, z: 4, core: 2. Of those that a mesh axis runs over, the one named last changes fastest.
Arguments:
- seq: float32 [768, 1024], P('row', 'col'), may hold values from -6 to 6
- query: float32 [768, 1024], P('row', 'col'), may hold values from -24 to 24, as said below
- key: float32 [768, 1024], P('col', 'row'), may hold values from -24 to 24, as said below
- value: float32 [768, 1024], P('col', 'row'), may hold values from -6 to 6
- pair: float32 [768, 768, 128], P('row', 'col'), may hold values from -6 to 6
- w_bias: float32 [128, 32], replicated, may hold values from -0.5 to 0.5
- w_out: float32 [1024, 1024], P(None, 'col'), may hold values from -0.75 to 0.75
- w_left: float32 [1024, 64], P('col'), may hold values from -0.1875 to 0.1875
- w_right: float32 [1024, 64], P('col'), may hold values from -0.1875 to 0.1875
- w_outer: float32 [128, 128], replicated, may hold values from -0.5 to 0.5
- outer_bias: float32 [128], replicated, may hold values from -3 to 3
- w_up: float32 [128, 512], replicated, may hold values from -0.5 to 0.5
- w_down: float32 [512, 128], replicated, may hold values from -0.25 to 0.25
Outputs:
- seq_new: float32 [768, 1024], P('row', 'col')
- pair_new: float32 [768, 768, 128], P('row', 'col')
Inputs may be any that keep to these rules, and one draw needn't show every extreme that they name: `query`: Head-major queries of order one; some residues may be much larger. `key`: Head-major keys of order one; some residues may be much larger.
All inputs are finite; a program needn't handle non-finite values.
Results may differ from a plain program's by a relative error of at most 0.0003.
Values sent between devices are 32-bit elements; how exact they have to be, the bound alone decides.
A program may use at most 128 MiB of HBM per device.

v0:
```python
import jax
import jax.numpy as jnp
from jax import lax
from jax.sharding import PartitionSpec as P

HIGH = lax.Precision.HIGHEST


def merged(x, axis, combine):
    everything = jax.tree.map(lambda part: lax.all_gather(part, axis), x)
    leading = jax.tree.map(lambda part: part[0], everything)

    def hop(k, so_far):
        return combine(so_far, jax.tree.map(lambda part: part[k], everything))

    return lax.fori_loop(1, lax.axis_size(axis), hop, leading)


def channel_norm(x):
    centre = x - jnp.mean(x, axis=-1, keepdims=True)
    return centre * lax.rsqrt(jnp.mean(centre * centre, axis=-1, keepdims=True) + 1e-05)


def combine(first, second):
    top = jnp.maximum(first[0], second[0])
    scale_one = jnp.exp(first[0] - top)
    scale_two = jnp.exp(second[0] - top)
    totals = first[1] * scale_one + second[1] * scale_two
    weighted = first[2] * scale_one[..., None] + second[2] * scale_two[..., None]
    return (top, totals, weighted)


def partial_softmax(q_heads, k_heads, v_heads, bias, scale):
    scores = jnp.einsum("ihd,jhd->ihj", q_heads, k_heads, precision=HIGH) * scale + bias
    top = jnp.max(scores, axis=2)
    expo = jnp.exp(scores - top[..., None])
    totals = jnp.sum(expo, axis=2)
    weighted = jnp.einsum("ihj,jhd->ihd", expo, v_heads, precision=HIGH)
    return (top, totals, weighted)


def per_device(
    seq, query, key, value, pair, w_bias, w_out, w_left, w_right, w_outer, outer_bias, w_up, w_down
):
    rows_here = pair.shape[0]
    cols_here = pair.shape[1]
    channels = pair.shape[2]
    heads = w_bias.shape[1]
    width = w_out.shape[0]
    head_dim = width // heads
    proj_width = w_left.shape[1]
    scale = 1.0 / jnp.sqrt(jnp.float32(head_dim))
    bias = jnp.einsum("ijc,ch->ihj", channel_norm(pair), w_bias, precision=HIGH)
    queries = lax.all_gather(query, "col", axis=1, tiled=True)
    keys_all, values_all = (
        lax.all_gather(key, "row", axis=1, tiled=True),
        lax.all_gather(value, "row", axis=1, tiled=True),
    )
    parts = partial_softmax(
        queries.reshape(rows_here, heads, head_dim),
        keys_all.reshape(cols_here, heads, head_dim),
        values_all.reshape(cols_here, heads, head_dim),
        bias,
        scale,
    )
    top, totals, weighted = merged(parts, "col", combine)
    attn = (weighted / totals[..., None]).reshape(rows_here, width)
    seq_new = seq + jnp.dot(attn, w_out, precision=HIGH)
    sum_value, sum_square = lax.psum(
        (jnp.sum(seq_new, axis=1), jnp.sum(seq_new * seq_new, axis=1)), "col"
    )
    mean_value = (sum_value / width)[:, None]
    mean_square = (sum_square / width)[:, None]
    seq_norm = (seq_new - mean_value) * lax.rsqrt(mean_square - mean_value * mean_value + 1e-05)
    left_part = jnp.dot(seq_norm, w_left, precision=HIGH)
    right_part = jnp.dot(seq_norm, w_right, precision=HIGH)
    left, right = lax.psum((left_part, right_part), "col")
    right_every = lax.all_gather(right, "row", axis=0, tiled=True)
    start = lax.axis_index("col") * cols_here
    right_block = lax.dynamic_slice_in_dim(right_every, start, cols_here, 0)
    w_prod = w_outer[:proj_width]
    w_diff = w_outer[proj_width:]
    table = right_block[:, :, None] * w_prod[None, :, :]
    left_diff = jnp.dot(left, w_diff, precision=HIGH)
    right_diff = jnp.dot(right_block, w_diff, precision=HIGH)
    outer = (
        jnp.einsum("ip,jpc->ijc", left, table, precision=HIGH)
        + left_diff[:, None, :]
        - right_diff[None, :, :]
        + outer_bias
    )
    pair_mid = pair + outer
    flat = pair_mid.reshape(rows_here * cols_here, channels)
    hidden_act = jax.nn.relu(jnp.dot(channel_norm(flat), w_up, precision=HIGH))
    pair_new = flat + jnp.dot(hidden_act, w_down, precision=HIGH)
    return (seq_new, pair_new.reshape(rows_here, cols_here, channels))


def solution(mesh):
    in_specs = (
        P("row", "col"),
        P("row", "col"),
        P("col", "row"),
        P("col", "row"),
        P("row", "col", None),
        P(),
        P(None, "col"),
        P("col", None),
        P("col", None),
        P(),
        P(),
        P(),
        P(),
    )
    out_specs = (P("row", "col"), P("row", "col", None))
    return jax.shard_map(
        per_device, mesh=mesh, in_specs=in_specs, out_specs=out_specs, check_vma=False
    )
```

profile of v0, /device:TPU:0, one launch (start us, length us, event | category | flops | bytes accessed | tf_op | source)
XLA Modules:
  0.0 294.8 jit_solution(9783816739350070599)
XLA Ops:
  7.2 0.0 copy-start
  7.2 0.0 all-gather.8.cloned.1.call-start
  7.2 0.7 all-gather.8.cloned.1.call-update
  7.9 0.0 all-gather.10.cloned.1.call-start
  8.0 0.7 all-gather.10.cloned.1.call-update
  8.7 6.7 %all_gather.31 = f32[48,1024]{1,0:T(8,128)S(1)} all-gather(f32[48,512]{1,0:T(8,128)} %param.14), channel_id=1, replica_groups=mesh['row'=16,'col'=2] {'col'}, dimensions={1}, use_global_device_ids=true | all-gather | bytes 294912 | tf_op jit(solution)/shard_map/all_gather | solution.py:54
  15.4 0.2 copy.49
  15.6 0.0 copy-start.7
  15.6 6.2 %reduce_sum.63 = f32[48,384]{1,0:T(8,128)S(1)} reduce(f32[48,384,128]{2,1,0:T(8,128)} %param.17, f32[]{:T(128)} %constant.13.clone.1), dimensions={2}, to_apply=%region_0.0 | reduce | flops 2340864 | bytes 9510916 | tf_op jit(solution)/shard_map/reduce_sum | solution.py:20
  21.8 7.9 %multiply_reduce_fusion.1 = f32[48,384]{1,0:T(8,128)S(1)} fusion(f32[48,384,128]{2,1,0:T(8,128)} %param.17, f32[48,384]{1,0:T(8,128)S(1)} %broadcast_multiply_fusion.1), kind=kLoop, calls=%fused_computation.12 | loop fusion | flops 7059456 | bytes 9584640 | tf_op jit(solution)/shard_map/reduce_sum | solution.py:21
  29.8 0.0 copy-done.7
  29.8 15.9 %fusion.9 = f32[48,384,32]{1,2,0:T(8,128)} fusion(f32[48,384,128]{2,1,0:T(8,128)} %param.17, f32[48,384]{1,0:T(8,128)S(1)} %add_rsqrt_fusion.1, f32[48,384]{1,0:T(8,128)S(1)} %broadcast_multiply_fusion.1, f32[128,32]{0,1:T(8,128)S(1)} %copy-done.7), kind=kOutput, calls=%fused_computation.10 | convolution fusion | flops 910688256 | bytes 11960320 | tf_op jit(solution)/shard_map/ijc,ch->ihj/dot_general | solution.py:53
  45.7 7.0 %all-gather.8.cloned.1.call-done = f32[384,1024]{0,1:T(8,128)} async-done(((f32[384,64]{0,1:T(8,128)}), f32[384,1024]{0,1:T(8,128)}) %all-gather.8.cloned.1.call-update) | async-done | bytes 1572880 | tf_op jit(solution)/shard_map/all_gather | solution.py:56
  52.6 5.7 %fusion.45 = (f32[48,32]{0,1:T(8,128)S(1)}, f32[48,32,384]{2,0,1:T(8,128)S(1)}) fusion(f32[48,384,32]{1,2,0:T(8,128)} %fusion.9, f32[384,32,32]{0,2,1:T(8,128)} %bitcast.72, f32[48,32,32]{0,2,1:T(8,128)S(1)} %bitcast.70), kind=kOutput, calls=%fused_computation.63 | convolution fusion | flops 228260352 | bytes 6494208 | tf_op jit(solution)/shard_map/ihd,jhd->ihj/dot_general | solution.py:34
  58.3 0.0 copy-start.4
  58.3 0.0 slice-start.6
  58.3 1.4 copy-done.2
  59.7 0.8 fusion.18
  60.5 32.8 %all-gather.10.cloned.1.call-done = f32[384,1024]{0,1:T(8,128)} async-done(((f32[384,64]{0,1:T(8,128)}), f32[384,1024]{0,1:T(8,128)}) %all-gather.10.cloned.1.call-update) | async-done | bytes 1572880 | tf_op jit(solution)/shard_map/all_gather | solution.py:57
  93.3 5.1 %fusion.20 = f32[48,32,32]{0,2,1:T(8,128)S(1)} fusion(f32[384,32,32]{0,2,1:T(8,128)} %bitcast.71, f32[48,32,384]{2,0,1:T(8,128)} %copy-done.2, f32[48,32]{0,1:T(8,128)S(1)} %get-tuple-element.37), kind=kOutput, calls=%fused_computation.22 | convolution fusion | flops 227082240 | bytes 4134912 | tf_op jit(solution)/shard_map/ihj,jhd->ihd/dot_general | solution.py:38
  98.4 4.4 %all-gather.3 = f32[2,48,32]{1,2,0:T(8,128)S(1)} all-gather(f32[1,48,32]{1,2,0:T(8,128)S(1)} %bitcast.73), channel_id=3, replica_groups=mesh['row'=16,'col'=2] {'col'}, dimensions={0}, use_global_device_ids=true | all-gather | bytes 18432 | tf_op jit(solution)/shard_map/all_gather | solution.py:10
  102.8 4.4 %all-gather.4 = f32[2,48,32]{1,2,0:T(8,128)S(1)} all-gather(f32[1,48,32]{1,2,0:T(8,128)S(1)} %bitcast.74), channel_id=4, replica_groups=mesh['row'=16,'col'=2] {'col'}, dimensions={0}, use_global_device_ids=true | all-gather | bytes 18432 | tf_op jit(solution)/shard_map/all_gather | solution.py:10
  107.2 0.1 copy.54
  107.3 0.1 copy.52
  107.4 0.7 copy.53
  108.1 0.7 copy.51
  108.8 0.0 copy-start.8
  108.8 18.0 %all-gather = f32[96,32,32]{2,1,0:T(8,128)S(1)} all-gather(f32[48,32,32]{2,1,0:T(8,128)S(1)} %copy.51), channel_id=2, replica_groups=mesh['row'=16,'col'=2] {'col'}, dimensions={0}, use_global_device_ids=true | all-gather | bytes 589824 | tf_op jit(solution)/shard_map/all_gather | solution.py:10
  126.8 1.6 fusion.23
  128.5 0.4 reshape.150
  128.9 0.0 copy-done
  128.9 2.3 fusion.42
  131.2 0.0 copy-start.3
  131.2 4.9 %all-reduce.1 = (f32[48]{0:T(128)S(1)}, f32[48]{0:T(128)S(1)}) all-reduce(f32[48]{0:T(128)S(1)} %get-tuple-element.19, f32[48]{0:T(128)S(1)} %get-tuple-element.18), channel_id=1, replica_groups=mesh['row'=16,'col'=2] {'col'}, use_global_device_ids=true, to_apply=%region_7.0 | all-reduce | flops 96 | bytes 768 | tf_op jit(solution)/shard_map/psum | solution.py:69
  136.2 1.2 fusion.24
  137.4 1.2 fusion.25
  138.6 8.6 %all-reduce = (f32[48,64]{1,0:T(8,128)S(1)}, f32[48,64]{1,0:T(8,128)S(1)}) all-reduce(f32[48,64]{1,0:T(8,128)S(1)} %fusion.24, f32[48,64]{1,0:T(8,128)S(1)} %fusion.25), channel_id=1, replica_groups=mesh['row'=16,'col'=2] {'col'}, use_global_device_ids=true, to_apply=%region_9.0 | all-reduce | flops 6144 | bytes 49152 | tf_op jit(solution)/shard_map/psum | solution.py:77
  147.2 0.0 copy-done.4
  147.2 0.2 fusion.32
  147.4 20.2 %all_gather.39 = f32[768,64]{1,0:T(8,128)S(1)} all-gather(f32[48,64]{1,0:T(8,128)S(1)} %get-tuple-element.20), channel_id=1, replica_groups=mesh['row'=16,'col'=2] {'row'}, dimensions={0}, use_global_device_ids=true | all-gather | bytes 208896 | tf_op jit(solution)/shard_map/all_gather | solution.py:78
  167.6 0.3 fusion.30
  167.9 0.0 slice-done.6
  167.9 0.0 copy-done.8
  167.9 22.6 %fusion.46 = (f32[48,384]{0,1:T(8,128)S(1)}, f32[48,384,128]{2,0,1:T(8,128)}) fusion(f32[128]{0:T(128)S(1)} %copy-done.8, f32[384,128]{1,0:T(8,128)S(1)} %fusion.30, f32[48,128]{1,0:T(8,128)S(1)} %fusion.32, f32[64,128]{1,0:T(8,128)S(1)} %slice-done.6, f32[384,64]{1,0:T(8,128)S(1)} %constant_dynamic-slice_fusion, f32[48,64]{1,0:T(8,128)S(1)} %get-tuple-element.21, ...), kind=kOutput, calls=%fused_computation.64 | convolution fusion | flops 1826863104 | bytes 19313152 | tf_op jit(solution)/shard_map/ip,jpc->ijc/dot_general | solution.py:87
  190.5 0.0 copy-done.3
  190.5 0.1 copy.57
  190.6 0.0 slice-start
  190.6 0.1 copy.58
  190.8 0.0 slice-start.1
  190.8 0.0 slice-start.2
  190.8 10.5 %copy.56 = f32[48,384,128]{2,1,0:T(8,128)} copy(f32[48,384,128]{2,0,1:T(8,128)} %get-tuple-element.41) | data formatting | bytes 18874368 | tf_op jit(solution)/shard_map/add | solution.py:92
  201.3 0.0 slice-done.2
  201.3 5.4 %multiply_reduce_fusion = f32[48,384]{0,1:T(8,128)S(1)} fusion(f32[48,384,128]{2,0,1:T(8,128)S(1)} %bitcast.65, f32[48,384]{0,1:T(8,128)S(1)} %copy.58), kind=kLoop, calls=%fused_computation.9 | loop fusion | flops 7059456 | bytes 9584640 | tf_op jit(solution)/shard_map/reduce_sum | solution.py:21
  206.7 0.1 copy.59
  206.9 0.0 copy-start.5
  206.9 0.0 slice-start.3
  206.9 11.4 %fusion.8 = f32[18432,128]{1,0:T(8,128)S(1)} fusion(f32[48,384,128]{2,1,0:T(8,128)} %copy.56, f32[18432]{0:T(1024)S(1)} %rsqrt.26, f32[18432]{0:T(1024)S(1)} %div.39), kind=kLoop, calls=%fused_computation.7 | loop fusion | flops 4718592 | bytes 19021824 | tf_op jit(solution)/shard_map/mul | solution.py:21
  218.3 0.0 copy-done.5
  218.3 0.0 slice-start.4
  218.3 0.0 slice-start.5
  218.3 0.0 copy-start.6
  218.3 33.8 %fusion.47 = f32[18432,512]{1,0:T(8,128)} fusion(f32[18432,128]{1,0:T(8,128)S(1)} %fusion.8, f32[128,512]{1,0:T(8,128)S(1)} %copy-done.5), kind=kOutput, calls=%fused_computation.65 | convolution fusion | flops 14495514624 | bytes 47448064 | tf_op jit(solution)/shard_map/dot_general | solution.py:94
  252.2 0.0 copy-start.1
  252.2 35.5 %fusion.2 = f32[18432,128]{1,0:T(8,128)} fusion(f32[18432,128]{1,0:T(8,128)S(1)} %bitcast.68, f32[512,128]{1,0:T(8,128)S(1)} %copy-done.6, f32[18432,512]{1,0:T(8,128)} %fusion.47), kind=kOutput, calls=%fused_computation.2 | convolution fusion | flops 14507311104 | bytes 56885248 | tf_op jit(solution)/shard_map/dot_general | solution.py:95
  (19 shorter events, 0.1 us)
Async XLA Ops:
  7.2 121.7 %copy-start = (f32[1024,512]{1,0:T(8,128)S(1)}, f32[1024,512]{1,0:T(8,128)}, u32[]{:S(2)}) copy-start(f32[1024,512]{1,0:T(8,128)} %param.19) | copy-start | bytes 6291460
  7.2 45.4 %all-gather.8.cloned.1.call-start = ((), (), s32[]{:S(2)}) async-start(), calls=%async_computation | async-start | bytes 1671168 | tf_op jit(solution)/shard_map/all_gather | solution.py:56
  7.9 85.4 %all-gather.10.cloned.1.call-start = ((), (), s32[]{:S(2)}) async-start(), calls=%async_computation.1 | async-start | bytes 1671168 | tf_op jit(solution)/shard_map/all_gather | solution.py:57
  15.6 14.2 %copy-start.7 = (f32[128,32]{0,1:T(8,128)S(1)}, f32[128,32]{0,1:T(8,128)}, u32[]{:S(2)}) copy-start(f32[128,32]{0,1:T(8,128)} %param.18) | copy-start | bytes 49156
  58.3 1.4 copy-start.2
  58.3 88.9 %copy-start.4 = (f32[128,128]{1,0:T(8,128)S(1)}, f32[128,128]{1,0:T(8,128)}, u32[]{:S(2)}) copy-start(f32[128,128]{1,0:T(8,128)} %param.22) | copy-start | bytes 196612
  58.3 109.6 %slice-start.6 = ((f32[128,128]{1,0:T(8,128)}), f32[64,128]{1,0:T(8,128)S(1)}, s32[]{:S(2)}) async-start(f32[128,128]{1,0:T(8,128)} %param.22), calls=%async_computation.8 | async-start | bytes 65536 | tf_op jit(solution)/shard_map/slice | solution.py:81
  108.8 59.1 %copy-start.8 = (f32[128]{0:T(128)S(1)}, f32[128]{0:T(128)}, u32[]{:S(2)}) copy-start(f32[128]{0:T(128)} %param.23) | copy-start | bytes 1540
  131.2 59.3 %copy-start.3 = (f32[48,512]{1,0:T(8,128)}, f32[48,512]{1,0:T(8,128)S(1)}, u32[]{:S(2)}) copy-start(f32[48,512]{1,0:T(8,128)S(1)} %get-tuple-element.39) | copy-start | bytes 294916
  190.6 10.6 %slice-start = ((s8[9437184]{0:T(1024)(128)(4,1)}), s8[1048576]{0:T(1024)(128)(4,1)S(1)}, s32[]{:S(2)}) async-start(s8[9437184]{0:T(1024)(128)(4,1)} %bitcast.64), calls=%async_computation.2 | async-start | bytes 2097152
  190.8 10.5 %slice-start.1 = ((s8[9437184]{0:T(1024)(128)(4,1)}), s8[4194304]{0:T(1024)(128)(4,1)S(1)}, s32[]{:S(2)}) async-start(s8[9437184]{0:T(1024)(128)(4,1)} %bitcast.64), calls=%async_computation.3 | async-start | bytes 8388608
  190.8 10.5 %slice-start.2 = ((s8[9437184]{0:T(1024)(128)(4,1)}), s8[4194304]{0:T(1024)(128)(4,1)S(1)}, s32[]{:S(2)}) async-start(s8[9437184]{0:T(1024)(128)(4,1)} %bitcast.64), calls=%async_computation.4 | async-start | bytes 8388608
  206.9 11.4 %copy-start.5 = (f32[128,512]{1,0:T(8,128)S(1)}, f32[128,512]{1,0:T(8,128)}, u32[]{:S(2)}) copy-start(f32[128,512]{1,0:T(8,128)} %param.24) | copy-start | bytes 786436
  206.9 45.3 %slice-start.3 = ((s8[9437184]{0:T(1024)(128)(4,1)}), s8[4194304]{0:T(1024)(128)(4,1)S(1)}, s32[]{:S(2)}) async-start(s8[9437184]{0:T(1024)(128)(4,1)} %bitcast.66), calls=%async_computation.5 | async-start | bytes 8388608
  218.3 33.9 %slice-start.4 = ((s8[9437184]{0:T(1024)(128)(4,1)}), s8[4194304]{0:T(1024)(128)(4,1)S(1)}, s32[]{:S(2)}) async-start(s8[9437184]{0:T(1024)(128)(4,1)} %bitcast.66), calls=%async_computation.6 | async-start | bytes 8388608
  218.3 33.9 %slice-start.5 = ((s8[9437184]{0:T(1024)(128)(4,1)}), s8[1048576]{0:T(1024)(128)(4,1)S(1)}, s32[]{:S(2)}) async-start(s8[9437184]{0:T(1024)(128)(4,1)} %bitcast.66), calls=%async_computation.7 | async-start | bytes 2097152
  218.3 33.9 %copy-start.6 = (f32[512,128]{1,0:T(8,128)S(1)}, f32[512,128]{1,0:T(8,128)}, u32[]{:S(2)}) copy-start(f32[512,128]{1,0:T(8,128)} %param.25) | copy-start | bytes 786436
  252.2 35.5 %copy-start.1 = (f32[1024,512]{1,0:T(8,128)S(1)}, f32[1024,512]{1,0:T(8,128)}, u32[]{:S(2)}) copy-start(f32[1024,512]{1,0:T(8,128)} %param.19) | copy-start | bytes 6291460
Sparse Core Ops, SparseCore 0:
  10.3 42.3 all-gather.7
  54.9 38.3 all-gather.9
where the time goes:
time: 298 us; the launch traced here: 295 us
  matrix products  124 us (42%)
  blocking collectives  67.2 us (23%)
  waiting for transfers between devices  41.1 us (14%)
  other arithmetic  33.5 us (11%)
  between operations  14.7 us (5%)
  local copies, waits for them, and re-layouts  14.4 us (5%)
    dot_general x1, matrix products, per_device(): pair_new = flat + jnp.dot(hidden_act, w_down, precision=HIGH)  35.5 us
    dot_general x1, matrix products, per_device(): hidden_act = jax.nn.relu(jnp.dot(channel_norm(flat), w_up, precision=HIGH))  33.8 us
    all_gather x1, waiting for transfers between devices, per_device(): lax.all_gather(value, 'row', axis=1, tiled=True)  32.8 us
    all_gather x3, blocking collectives, merged(): everything = jax.tree.map(lambda part: lax.all_gather(part, axis), x)  26.8 us
    dot_general x1, matrix products, per_device(): jnp.einsum('ip,jpc->ijc', left, table, precision=HIGH)  22.6 us
    all_gather x1, blocking collectives, per_device(): right_every = lax.all_gather(right, 'row', axis=0, tiled=True)  20.2 us
    dot_general x1, matrix products, per_device(): bias = jnp.einsum('ijc,ch->ihj', channel_norm(pair), w_bias, precision=HIGH)  15.9 us
    reduce_sum x2, other arithmetic, channel_norm(): jnp.mean(centre * centre, axis=-1, keepdims=True) + 1e-05  13.4 us
  transfers between devices with their start and end apart: 2, of which 2 were waited for; matrix products, arithmetic and copies ran while one was open for 12% of the time, Pallas kernels for 0%

commit v1 on v0

v1 whole, which is shorter than its diff:
```python
import functools

import jax
import jax.numpy as jnp
from jax import lax
from jax.experimental import pallas as pl
from jax.experimental.pallas import tpu as pltpu
from jax.sharding import PartitionSpec as P

HIGH = lax.Precision.HIGHEST
F32 = jnp.float32
BF16 = jnp.bfloat16
VMEM_LIMIT = 60 * 1024 * 1024


def halves(x):
    high = x.astype(BF16)
    low = (x - high.astype(F32)).astype(BF16)
    return high, low


def split(x):
    kept = lax.reduce_precision(x, 8, 7)
    return kept.astype(BF16), (x - kept).astype(BF16)


def channel_norm(x):
    centre = x - jnp.mean(x, axis=-1, keepdims=True)
    return centre * lax.rsqrt(jnp.mean(centre * centre, axis=-1, keepdims=True) + 1e-05)


def dot_nt(a, b, precision=None):
    return lax.dot_general(
        a, b, (((1,), (1,)), ((), ())), precision=precision, preferred_element_type=F32
    )


def bias_kernel(pair_ref, wt_hi_ref, wt_lo_ref, out_ref):
    group = pair_ref.shape[0]
    rows = [halves(channel_norm(pair_ref[i])) for i in range(group)]
    high = jnp.concatenate([r[0] for r in rows], axis=1)
    low = jnp.concatenate([r[1] for r in rows], axis=1)
    wt_hi = wt_hi_ref[...]
    flat = dot_nt(wt_hi, high) + (dot_nt(wt_hi, low) + dot_nt(wt_lo_ref[...], high))
    out_ref[...] = flat.reshape(out_ref.shape)


def pair_bias(pair, w_bias):
    rows, cols, channels = pair.shape
    heads = w_bias.shape[1]
    group = 8
    eye = jnp.eye(group, dtype=F32)
    wt = (w_bias.T[:, None, None, :] * eye[None, :, :, None]).reshape(
        heads * group, group * channels
    )
    wt_hi, wt_lo = split(wt)
    whole = pl.BlockSpec((heads * group, group * channels), lambda i: (0, 0))
    return pl.pallas_call(
        bias_kernel,
        out_shape=jax.ShapeDtypeStruct((heads, rows, cols), F32),
        grid=(rows // group,),
        in_specs=[pl.BlockSpec((group, cols, channels), lambda i: (i, 0, 0)), whole, whole],
        out_specs=pl.BlockSpec((heads, group, cols), lambda i: (0, i, 0)),
        compiler_params=pltpu.CompilerParams(vmem_limit_bytes=VMEM_LIMIT),
        name="pair_bias",
    )(pair, wt_hi, wt_lo)


def attention_kernel(head_dim, q_ref, k_ref, v_ref, bias_ref, part_ref, top_ref, total_ref):
    rows = q_ref.shape[0]
    heads = bias_ref.shape[0]
    per = 128 // head_dim
    scale = F32(head_dim) ** -0.5
    lane = lax.broadcasted_iota(jnp.int32, (rows, 128), 1)
    tops = jnp.zeros((rows, 128), F32)
    totals = jnp.zeros((rows, 128), F32)
    for g in range(heads // per):
        lanes = slice(g * 128, (g + 1) * 128)
        q = q_ref[:, lanes]
        q4 = jnp.concatenate(
            [jnp.where(lane // head_dim == m, q, 0.0) for m in range(per)], axis=0
        )
        bias = bias_ref[g * per : (g + 1) * per].reshape(per * rows, -1)
        scores = dot_nt(q4, k_ref[:, lanes], HIGH) * scale + bias
        top = jnp.max(scores, axis=1, keepdims=True)
        expo = jnp.exp(scores - top)
        total = jnp.sum(expo, axis=1, keepdims=True)
        e_hi, e_lo = halves(expo)
        v_hi, v_lo = halves(v_ref[:, lanes])
        dot = functools.partial(jnp.dot, preferred_element_type=F32)
        out = dot(e_hi, v_hi) + (dot(e_hi, v_lo) + dot(e_lo, v_hi))
        part = jnp.zeros((rows, 128), F32)
        for m in range(per):
            mine = slice(m * rows, (m + 1) * rows)
            part = jnp.where(lane // head_dim == m, out[mine], part)
            tops = jnp.where(lane == g * per + m, top[mine], tops)
            totals = jnp.where(lane == g * per + m, total[mine], totals)
        part_ref[:, lanes] = part
    top_ref[...] = tops
    total_ref[...] = totals


def attention(q, k, v, bias, head_dim):
    rows, width = q.shape
    small = jax.ShapeDtypeStruct((rows, 128), F32)
    return pl.pallas_call(
        functools.partial(attention_kernel, head_dim),
        out_shape=(jax.ShapeDtypeStruct((rows, width), F32), small, small),
        compiler_params=pltpu.CompilerParams(vmem_limit_bytes=VMEM_LIMIT),
        name="attention",
    )(q, k, v, bias)


def transition_kernel(
    pair_ref, left_ref, right_ref, w_outer_ref, bias_ref, up_ref, down_ref, down_hi_ref, out_ref,
    left_t, right_s, left_d,
):
    step = pl.program_id(0)
    group, cols, channels = pair_ref.shape
    proj = left_ref.shape[1]
    dot = functools.partial(jnp.dot, preferred_element_type=F32)

    @pl.when(step == 0)
    def _():
        left = left_ref[...]
        left_t[...] = left.T
        left_d[...] = jnp.dot(left, w_outer_ref[proj:], precision=HIGH) + bias_ref[...]
        r_hi, r_lo = halves(right_ref[...])
        right_s[...] = jnp.concatenate([r_hi, r_lo, r_hi], axis=1)

    lane = lax.broadcasted_iota(jnp.int32, left_t.shape, 1)
    w_prod = w_outer_ref[:proj]
    w_diff = w_outer_ref[proj:]
    weights = []
    for g in range(group):
        column = jnp.sum(
            jnp.where(lane == step * group + g, left_t[...], 0.0), axis=1, keepdims=True
        )
        w_hi, w_lo = halves(column * w_prod - w_diff)
        weights.append(jnp.concatenate([w_hi, w_hi, w_lo], axis=0))
    outer = dot(right_s[...], jnp.concatenate(weights, axis=1))
    for g in range(group):
        mid = pair_ref[g] + (
            outer[:, g * channels : (g + 1) * channels]
            + left_d[pl.ds(step * group + g, 1), :]
        )
        x_hi, x_lo = halves(channel_norm(mid))
        hidden = jnp.maximum(dot(jnp.concatenate([x_hi, x_lo, x_hi], axis=1), up_ref[...]), 0.0)
        h_hi, h_lo = halves(hidden)
        both = dot(h_hi, down_ref[...])
        out_ref[g] = mid + (
            both[:, :channels] + (both[:, channels:] + dot(h_lo, down_hi_ref[...]))
        )


def transition(pair, left, right, w_outer, outer_bias, w_up, w_down):
    rows, cols, channels = pair.shape
    proj = left.shape[1]
    hidden = w_up.shape[1]
    group = 2
    up_hi, up_lo = split(w_up)
    up = jnp.concatenate([up_hi, up_hi, up_lo], axis=0)
    down_hi, down_lo = split(w_down)
    down = jnp.concatenate([down_hi, down_lo], axis=1)

    def whole(x):
        return pl.BlockSpec(x.shape, lambda i: (0,) * x.ndim)

    block = pl.BlockSpec((group, cols, channels), lambda i: (i, 0, 0))
    fixed = (left, right, w_outer, outer_bias.reshape(1, channels), up, down, down_hi)
    return pl.pallas_call(
        transition_kernel,
        out_shape=jax.ShapeDtypeStruct(pair.shape, F32),
        grid=(rows // group,),
        in_specs=[block] + [whole(x) for x in fixed],
        out_specs=block,
        scratch_shapes=[
            pltpu.VMEM((proj, rows), F32),
            pltpu.VMEM((cols, 3 * proj), BF16),
            pltpu.VMEM((rows, channels), F32),
        ],
        compiler_params=pltpu.CompilerParams(vmem_limit_bytes=VMEM_LIMIT),
        name="transition",
    )(pair, *fixed)


def per_device(
    seq, query, key, value, pair, w_bias, w_out, w_left, w_right, w_outer, outer_bias, w_up, w_down
):
    rows, cols, channels = pair.shape
    heads = w_bias.shape[1]
    width = w_out.shape[0]
    head_dim = width // heads
    proj = w_left.shape[1]
    queries = lax.all_gather(query, "col", axis=1, tiled=True)
    keys = lax.all_gather(key, "row", axis=1, tiled=True)
    values = lax.all_gather(value, "row", axis=1, tiled=True)
    bias = pair_bias(pair, w_bias)
    part, top, total = attention(queries, keys, values, bias, head_dim)
    every = lax.all_gather(
        jnp.concatenate([part, top[:, :heads], total[:, :heads]], axis=1), "col"
    )
    parts = every[:, :, :width]
    tops = every[:, :, width : width + heads]
    totals = every[:, :, width + heads :]
    scale = jnp.exp(tops - jnp.max(tops, axis=0))
    scale = scale / jnp.sum(scale * totals, axis=0)
    attn = jnp.sum(parts * jnp.repeat(scale, head_dim, axis=2), axis=0)
    seq_new = seq + jnp.dot(attn, w_out, precision=HIGH)
    here = seq.shape[1]
    local_mean = jnp.mean(seq_new, axis=1, keepdims=True)
    centred = seq_new - local_mean
    w_both = jnp.concatenate([w_left, w_right], axis=1)
    projected = jnp.dot(centred, w_both, precision=HIGH)
    spread = jnp.sum(centred * centred, axis=1, keepdims=True)
    column = jnp.broadcast_to(jnp.sum(w_both, axis=0, keepdims=True), (rows, 2 * proj))
    sent = jnp.concatenate([projected, column, local_mean, spread], axis=1)
    every = lax.all_gather(sent, "col")
    means = every[:, :, 4 * proj : 4 * proj + 1]
    spreads = every[:, :, 4 * proj + 1 :]
    mean = jnp.mean(means, axis=0)
    offset = means - mean
    variance = (jnp.sum(spreads, axis=0) + here * jnp.sum(offset * offset, axis=0)) / width
    both = jnp.sum(every[:, :, : 2 * proj] + offset * every[:, :, 2 * proj : 4 * proj], axis=0)
    both = both * lax.rsqrt(variance + 1e-05)
    left = both[:, :proj]
    right_every = lax.all_gather(both[:, proj:], "row", axis=0, tiled=True)
    right = lax.dynamic_slice_in_dim(right_every, lax.axis_index("col") * cols, cols, 0)
    pair_new = transition(pair, left, right, w_outer, outer_bias, w_up, w_down)
    return seq_new, pair_new


def solution(mesh):
    in_specs = (
        P("row", "col"),
        P("row", "col"),
        P("col", "row"),
        P("col", "row"),
        P("row", "col", None),
        P(),
        P(None, "col"),
        P("col", None),
        P("col", None),
        P(),
        P(),
        P(),
        P(),
    )
    out_specs = (P("row", "col"), P("row", "col", None))
    return jax.shard_map(
        per_device, mesh=mesh, in_specs=in_specs, out_specs=out_specs, check_vma=False
    )
```

time: 298 us -> 194 us (0.65)
  matrix products: 124 us -> 1.87 us
  Pallas kernels: 0 us -> 60.9 us
  other arithmetic: 33.5 us -> 4.46 us
  blocking collectives: 67.2 us -> 39.9 us
  waiting for transfers between devices: 41.1 us -> 58 us
    dot_general x10 -> x1, matrix products: 121 us -> 0.42 us  [per_device(): projected = jnp.dot(centred, w_both, precision=HIGH)]
    pallas_call x0 -> x3, Pallas kernels: none -> 60.9 us  [the longest x1 39.7 us: transition(): pl.pallas_call(transition_kernel, out_shape=jax.ShapeDtypeStruct(pair.sha...]
    reduce_sum x4 -> x7, other arithmetic: 20.4 us -> 0.69 us  [the longest x1 0.18 us: per_device(): spread = jnp.sum(centred * centred, axis=1, keepdims=True)]
    all_gather x2, waiting for transfers between devices: 39.8 us -> 56.6 us  [the longest x1 37.6 us: per_device(): values = lax.all_gather(value, 'row', axis=1, tiled=True)]
    all_gather x4 -> x3, blocking collectives: 47 us -> 33.4 us  [the longest x1 20.2 us: per_device(): right_every = lax.all_gather(both[:, proj:], 'row', axis=0, tiled=True)]
    psum x2 -> x0, blocking collectives: 13.5 us -> none  [the longest x1 8.59 us: per_device(): left, right = lax.psum((left_part, right_part), 'col')]
    mul x1, other arithmetic: 11.4 us -> 0.07 us  [per_device(): both = both * lax.rsqrt(variance + 1e-05)]
    add x2 -> x0, local copies, waits for them, and re-layouts: 10.5 us -> none  [the longest x1 10.5 us: per_device(): pair_mid = pair + outer]
  transfers between devices with their start and end apart: 2 -> 2, of which waited for: 2 -> 2; matrix products, arithmetic and copies ran while one was open for 12% -> 4% of each run, Pallas kernels for 0% -> 7%
where the time goes in v1:
time: 194 us
  Pallas kernels  60.9 us (31%)
  waiting for transfers between devices  58 us (30%)
  blocking collectives  39.9 us (21%)
  local copies, waits for them, and re-layouts  14.2 us (7%)
  between operations  14.2 us (7%)
  other arithmetic  4.46 us (2%)
    pallas_call x1, Pallas kernels, transition(): pl.pallas_call(transition_kernel, out_shape=jax.ShapeDtypeStruct(pair.sha...  39.7 us
    all_gather x1, waiting for transfers between devices, per_device(): values = lax.all_gather(value, 'row', axis=1, tiled=True)  37.6 us
    all_gather x1, blocking collectives, per_device(): right_every = lax.all_gather(both[:, proj:], 'row', axis=0, tiled=True)  20.2 us
    all_gather x1, waiting for transfers between devices, per_device(): keys = lax.all_gather(key, 'row', axis=1, tiled=True)  19 us
    pallas_call x1, Pallas kernels, pair_bias(): pl.pallas_call(bias_kernel, out_shape=jax.ShapeDtypeStruct((heads, rows,...  12.9 us
    pallas_call x1, Pallas kernels, attention(): pl.pallas_call(functools.partial(attention_kernel, head_dim), out_shape=(...  8.35 us
    all_gather x1, blocking collectives, per_device(): lax.all_gather(jnp.concatenate([part, top[:, :heads], total[:, :heads]],...  8.21 us
    all_gather x1, blocking collectives, per_device(): queries = lax.all_gather(query, 'col', axis=1, tiled=True)  6.51 us
  transfers between devices with their start and end apart: 2, of which 2 were waited for; matrix products, arithmetic and copies ran while one was open for 4% of the time, Pallas kernels for 7%

profile of v1, /device:TPU:0, one launch (start us, length us, event | category | flops | bytes accessed | tf_op | source)
XLA Modules:
  0.0 193.6 jit_solution(2634556805083197764)
XLA Ops:
  7.2 0.0 copy-start
  7.2 0.0 all-gather.5.cloned.1.call-start
  7.2 0.7 all-gather.5.cloned.1.call-update
  7.9 0.0 all-gather.7.cloned.1.call-start
  8.0 0.7 all-gather.7.cloned.1.call-update
  8.7 0.9 constant_dynamic-update-slice_fusion.1
  9.6 0.9 constant_dynamic-update-slice_fusion
  10.5 0.1 reduce_sum.84
  10.6 2.0 %fusion = (bf16[256,1024]{1,0:T(8,128)(2,1)}, bf16[256,1024]{1,0:T(8,128)(2,1)}) fusion(f32[8,8]{0,1:T(8,128)S(1)} %fusion.11, f32[32,128]{1,0:T(8,128)} %bitcast.27), kind=kLoop, calls=%fused_computation.3 | loop fusion | flops 1310720 | bytes 1065216 | tf_op jit(solution)/shard_map/convert_element_type | solution.py:24
  12.6 0.0 copy-start.6
  12.6 0.0 copy-start.3
  12.6 0.0 copy-start.4
  12.6 12.9 %pair_bias.1.bias_ref = f32[32,48,384]{2,1,0:T(8,128)} custom-call(f32[48,384,128]{2,1,0:T(8,128)} %pair_ref.3, bf16[256,1024]{1,0:T(8,128)(2,1)} %get-tuple-element.18.wt_hi_ref, bf16[256,1024]{1,0:T(8,128)(2,1)} %get-tuple-element.17.wt_lo_ref), custom_call_target="tpu_custom_call" | custom-call | tf_op jit(solution)/shard_map/pair_bias/pallas_call | solution.py:58
  25.5 0.0 copy-done.6
  25.5 6.5 %all_gather.24.q_ref = f32[48,1024]{1,0:T(8,128)} all-gather(f32[48,512]{1,0:T(8,128)S(1)} %copy-done.6), channel_id=1, replica_groups=mesh['row'=16,'col'=2] {'col'}, dimensions={1}, use_global_device_ids=true | all-gather | bytes 294912 | tf_op jit(solution)/shard_map/all_gather | solution.py:195
  32.0 0.0 copy-done.3
  32.1 0.0 copy-start.1
  32.1 0.7 pad_maximum_fusion.1.down_ref
  32.8 0.0 copy-done.4
  32.8 0.8 pad_maximum_fusion.up_ref
  33.6 19.0 %all-gather.5.cloned.1.call-done = f32[384,1024]{0,1:T(8,128)} async-done(((f32[384,64]{0,1:T(8,128)}), f32[384,1024]{0,1:T(8,128)}) %all-gather.5.cloned.1.call-update) | async-done | bytes 1572880 | tf_op jit(solution)/shard_map/all_gather | solution.py:196
  52.6 3.0 %copy.25.k_ref = f32[384,1024]{1,0:T(8,128)} copy(f32[384,1024]{0,1:T(8,128)} %all-gather.5.cloned.1.call-done) | data formatting | bytes 3145728 | tf_op jit(solution)/shard_map/all_gather | solution.py:196
  55.6 0.0 copy-done.1
  55.6 37.6 %all-gather.7.cloned.1.call-done = f32[384,1024]{0,1:T(8,128)} async-done(((f32[384,64]{0,1:T(8,128)}), f32[384,1024]{0,1:T(8,128)}) %all-gather.7.cloned.1.call-update) | async-done | bytes 1572880 | tf_op jit(solution)/shard_map/all_gather | solution.py:197
  93.2 3.0 %copy.26.v_ref = f32[384,1024]{1,0:T(8,128)} copy(f32[384,1024]{0,1:T(8,128)} %all-gather.7.cloned.1.call-done) | data formatting | bytes 3145728 | tf_op jit(solution)/shard_map/all_gather | solution.py:197
  96.3 8.3 %attention.1 = (f32[48,1024]{1,0:T(8,128)}, f32[48,128]{1,0:T(8,128)}, f32[48,128]{1,0:T(8,128)}) custom-call(f32[48,1024]{1,0:T(8,128)} %all_gather.24.q_ref, f32[384,1024]{1,0:T(8,128)} %copy.25.k_ref, f32[384,1024]{1,0:T(8,128)} %copy.26.v_ref, f32[32,48,384]{2,1,0:T(8,128)} %pair_bias.1.bias_ref), custom_call_target="tpu_custom_call" | custom-call | tf_op jit(solution)/shard_map/attention/pallas_call | solution.py:106
  104.6 1.0 concatenate.15
  105.6 8.2 %all-gather = f32[96,1088]{1,0:T(8,128)S(1)} all-gather(f32[48,1088]{1,0:T(8,128)S(1)} %concatenate.15), channel_id=2, replica_groups=mesh['row'=16,'col'=2] {'col'}, dimensions={0}, use_global_device_ids=true | all-gather | bytes 626688 | tf_op jit(solution)/shard_map/all_gather | solution.py:200
  113.9 0.1 fusion.8
  114.0 0.0 copy-start.5
  114.0 1.6 broadcast_in_dim.6
  115.6 2.1 %reshape.61 = f32[2,48,1024]{2,1,0:T(8,128)S(1)} reshape(f32[2,48,32,32]{3,2,1,0:T(8,128)} %broadcast_in_dim.6) | data formatting | bytes 786432 | tf_op jit(solution)/shard_map/reshape | solution.py:208
  117.8 0.0 copy-done
  117.8 0.0 copy-done.5
  117.8 1.4 fusion.14
  119.2 0.0 copy-start.2
  119.3 0.4 fusion.4
  119.7 0.2 multiply_reduce_fusion
  119.9 0.1 copy.28
  120.0 0.1 copy.27
  120.1 0.1 pad_maximum_fusion.2
  120.1 5.0 %all-gather.1 = f32[96,258]{1,0:T(8,128)S(1)} all-gather(f32[48,258]{1,0:T(8,128)S(1)} %pad_maximum_fusion.2), channel_id=3, replica_groups=mesh['row'=16,'col'=2] {'col'}, dimensions={0}, use_global_device_ids=true | all-gather | bytes 148608 | tf_op jit(solution)/shard_map/all_gather | solution.py:218
  125.1 0.2 slice_reduce_fusion
  125.3 0.1 copy.30
  125.4 0.1 fusion.7
  125.5 0.1 broadcast_multiply_fusion
  125.6 0.6 fusion.13
  126.2 20.2 %all_gather.31 = f32[768,64]{1,0:T(8,128)S(1)} all-gather(f32[48,64]{1,0:T(8,128)S(1)} %get-tuple-element.15), channel_id=1, replica_groups=mesh['row'=16,'col'=2] {'row'}, dimensions={0}, use_global_device_ids=true | all-gather | bytes 208896 | tf_op jit(solution)/shard_map/all_gather | solution.py:227
  146.4 0.7 constant_dynamic-slice_fusion.right_ref
  147.1 39.7 %transition.1 = f32[48,384,128]{2,1,0:T(8,128)} custom-call(f32[48,384,128]{2,1,0:T(8,128)} %pair_ref.3, f32[48,64]{1,0:T(8,128)} %get-tuple-element.16.left_ref, f32[384,64]{1,0:T(8,128)} %constant_dynamic-slice_fusion.right_ref, f32[128,128]{1,0:T(8,128)} %w_outer_ref.1, f32[1,128]{1,0:T(1,128)} %bitcast.29, bf16[384,512]{1,0:T(8,128)(2,1)} %pad_maximum_fusion.up_ref, ...), custom_call_target="tpu_custom_call" | custom-call | tf_op jit(solution)/shard_map/transition/pallas_call | solution.py:171
  186.8 0.0 copy-done.2
  (11 shorter events, 0.2 us)
Async XLA Ops:
  7.2 110.6 %copy-start = (f32[1024,512]{1,0:T(8,128)S(1)}, f32[1024,512]{1,0:T(8,128)}, u32[]{:S(2)}) copy-start(f32[1024,512]{1,0:T(8,128)} %param.19) | copy-start | bytes 6291460
  7.2 45.4 %all-gather.5.cloned.1.call-start = ((), (), s32[]{:S(2)}) async-start(), calls=%async_computation | async-start | bytes 1671168 | tf_op jit(solution)/shard_map/all_gather | solution.py:196
  7.9 85.3 %all-gather.7.cloned.1.call-start = ((), (), s32[]{:S(2)}) async-start(), calls=%async_computation.1 | async-start | bytes 1671168 | tf_op jit(solution)/shard_map/all_gather | solution.py:197
  12.6 12.9 %copy-start.6 = (f32[48,512]{1,0:T(8,128)S(1)}, f32[48,512]{1,0:T(8,128)}, u32[]{:S(2)}) copy-start(f32[48,512]{1,0:T(8,128)} %param.14) | copy-start | bytes 294916
  12.6 19.4 %copy-start.3 = (f32[512,128]{1,0:T(8,128)S(1)}, f32[512,128]{1,0:T(8,128)}, u32[]{:S(2)}) copy-start(f32[512,128]{1,0:T(8,128)} %param.25) | copy-start | bytes 786436
  12.6 20.2 %copy-start.4 = (f32[128,512]{1,0:T(8,128)S(1)}, f32[128,512]{1,0:T(8,128)}, u32[]{:S(2)}) copy-start(f32[128,512]{1,0:T(8,128)} %param.24) | copy-start | bytes 786436
  32.1 23.6 %copy-start.1 = (bf16[512,128]{1,0:T(8,128)(2,1)}, bf16[512,128]{1,0:T(8,128)(2,1)S(1)}, u32[]{:S(2)}) copy-start(bf16[512,128]{1,0:T(8,128)(2,1)S(1)} %get-tuple-element.10.down_hi_ref) | copy-start | bytes 393220
  114.0 3.8 %copy-start.5 = (f32[48,512]{1,0:T(8,128)S(1)}, f32[48,512]{1,0:T(8,128)}, u32[]{:S(2)}) copy-start(f32[48,512]{1,0:T(8,128)} %param.13) | copy-start | bytes 294916
  119.2 67.5 %copy-start.2 = (f32[48,512]{1,0:T(8,128)}, f32[48,512]{1,0:T(8,128)S(1)}, u32[]{:S(2)}) copy-start(f32[48,512]{1,0:T(8,128)S(1)} %get-tuple-element.24) | copy-start | bytes 294916
Sparse Core Ops, SparseCore 0:
  10.3 42.2 all-gather.4
  54.9 38.2 all-gather.6

commit v2 on v1

--- a/solution.py
+++ b/solution.py
@@ -11,6 +11,7 @@
 F32 = jnp.float32
 BF16 = jnp.bfloat16
 VMEM_LIMIT = 60 * 1024 * 1024
+MESH = pl.DeviceIdType.MESH
 
 
 def halves(x):
@@ -35,80 +36,221 @@
     )
 
 
-def bias_kernel(pair_ref, wt_hi_ref, wt_lo_ref, out_ref):
-    group = pair_ref.shape[0]
-    rows = [halves(channel_norm(pair_ref[i])) for i in range(group)]
-    high = jnp.concatenate([r[0] for r in rows], axis=1)
-    low = jnp.concatenate([r[1] for r in rows], axis=1)
-    wt_hi = wt_hi_ref[...]
-    flat = dot_nt(wt_hi, high) + (dot_nt(wt_hi, low) + dot_nt(wt_lo_ref[...], high))
-    out_ref[...] = flat.reshape(out_ref.shape)
-
-
-def pair_bias(pair, w_bias):
+def gather_attention_kernel(
+    n, n_col, head_dim, heads,
+    kv_ref, q_ref, pair_ref, wt_hi_ref, wt_lo_ref,
+    part_ref, stat_ref,
+    kv_buf, q_buf, bias_buf, pair_buf,
+    recv_sem, z_sem, y_sem, core_sem, q_send, q_recv, pair_sem,
+):
+    n_z = n // 4
+    n_slot, rows, wide = q_ref.shape
+    groups, group = pair_buf.shape[:2]
+    per = wide // 2 // head_dim
+    row, col = lax.axis_index("row"), lax.axis_index("col")
+    core, y = lax.rem(row, 2), lax.rem(lax.div(row, 2), 2)
+    core_peer, y_peer = row + 1 - 2 * core, row + 2 - 4 * y
+    z_peers = [lax.rem(row + 4 * k, n) for k in range(1, n_z)]
+    col_peers = [lax.rem(col + k, n_col) for k in range(1, n_col)]
+
+    def pair_copy(g):
+        return pltpu.make_async_copy(
+            pair_ref.at[pl.ds(g * group, group)], pair_buf.at[g], pair_sem.at[g]
+        )
+
+    for g in range(groups):
+        pair_copy(g).start()
+    own_kv = pltpu.make_async_copy(kv_ref, kv_buf.at[row], recv_sem.at[row])
+    own_kv.start()
+    own_q = pltpu.make_async_copy(
+        q_ref, q_buf.at[pl.ds(col * n_slot, n_slot)], q_recv.at[col]
+    )
+    own_q.start()
+
+    barrier = pltpu.get_barrier_semaphore()
+    for peer in z_peers + [y_peer, core_peer]:
+        pl.semaphore_signal(barrier, inc=1, device_id={"row": peer}, device_id_type=MESH)
+    for peer in col_peers:
+        pl.semaphore_signal(barrier, inc=1, device_id={"col": peer}, device_id_type=MESH)
+    pl.semaphore_wait(barrier, n_z + n_col)
+
+    def put(src, slot, sem, peer):
+        return pltpu.make_async_remote_copy(
+            src_ref=src,
+            dst_ref=kv_buf.at[slot],
+            send_sem=sem,
+            recv_sem=recv_sem.at[slot],
+            device_id={"row": peer},
+            device_id_type=MESH,
+        )
+
+    def put_q(slot_col, peer, sem):
+        return pltpu.make_async_remote_copy(
+            src_ref=q_ref,
+            dst_ref=q_buf.at[pl.ds(slot_col * n_slot, n_slot)],
+            send_sem=sem,
+            recv_sem=q_recv.at[slot_col],
+            device_id={"col": peer},
+            device_id_type=MESH,
+        )
+
+    order = [0]
+    for k in range(1, n_z // 2 + 1):
+        order += [k] if 2 * k == n_z else [k, n_z - k]
+    put(kv_ref, row, y_sem.at[0], y_peer).start()
+    for t in range(1, n_z):
+        put(kv_ref, row, z_sem.at[t], z_peers[order[t] - 1]).start()
+    put(kv_ref, row, core_sem.at[0], core_peer).start()
+    for k, peer in enumerate(col_peers):
+        put_q(col, peer, q_send.at[k]).start()
+    own_kv.wait()
+    own_q.wait()
+
+    def slot_z(t):
+        return lax.rem(row - 4 * order[t] + n, n)
+
+    def relay_z(t):
+        slot = slot_z(t)
+        put(kv_buf.at[slot], slot, y_sem.at[t], y_peer).wait_recv()
+        put(kv_buf.at[slot], slot, y_sem.at[t], y_peer).start()
+        put(kv_buf.at[slot], slot, core_sem.at[2 * t], core_peer).start()
+
+    def relay_y(t):
+        slot = slot_z(t) + 2 - 4 * y
+        put(kv_buf.at[slot], slot, core_sem.at[2 * t + 1], core_peer).wait_recv()
+        put(kv_buf.at[slot], slot, core_sem.at[2 * t + 1], core_peer).start()
+
+    def bias_group(g, carry):
+        pair_copy(g).wait()
+        parts = [halves(channel_norm(pair_buf[g, i])) for i in range(group)]
+        high = jnp.concatenate([p[0] for p in parts], axis=1)
+        low = jnp.concatenate([p[1] for p in parts], axis=1)
+        wt_hi = wt_hi_ref[...]
+        flat = dot_nt(wt_hi, high) + (dot_nt(wt_hi, low) + dot_nt(wt_lo_ref[...], high))
+        bias_buf[:, pl.ds(pl.multiple_of(g * group, group), group), :] = flat.reshape(
+            heads, group, flat.shape[1]
+        )
+        return carry
+
+    for t in range(1, n_z):
+        lax.fori_loop(
+            (t - 1) * groups // (n_z - 1), t * groups // (n_z - 1), bias_group, 0
+        )
+        relay_z(t)
+        relay_y(t - 1)
+    for k in range(1, n_col):
+        source = lax.rem(col - k + n_col, n_col)
+        put_q(source, col_peers[k - 1], q_send.at[k - 1]).wait_recv()
+
+    scale = F32(head_dim) ** -0.5
+    lane = lax.broadcasted_iota(jnp.int32, (rows, wide), 1) // head_dim
+    stat_lane = lax.broadcasted_iota(jnp.int32, (rows, stat_ref.shape[2]), 1)
+    dot = functools.partial(jnp.dot, preferred_element_type=F32)
+    stat_ref[...] = jnp.zeros_like(stat_ref)
+
+    def attend(base):
+        part = jnp.zeros((rows, wide), F32)
+        for par in range(2):
+            slot = base + par
+            k_at, v_at = (per, 0) if par == 0 else (0, per)
+            q = q_buf[slot]
+            kv = kv_buf[slot]
+            qs = jnp.concatenate(
+                [jnp.where(lane == k_at + m, q, 0.0) for m in range(per)], axis=0
+            )
+            bias = bias_buf[pl.ds(slot * per, per)].reshape(per * rows, -1)
+            scores = dot_nt(qs, kv, HIGH) * scale + bias
+            top = jnp.max(scores, axis=1, keepdims=True)
+            expo = jnp.exp(scores - top)
+            total = jnp.sum(expo, axis=1, keepdims=True)
+            e_hi, e_lo = halves(expo)
+            v_hi, v_lo = halves(kv)
+            out = dot(e_hi, v_hi) + (dot(e_hi, v_lo) + dot(e_lo, v_hi))
+            for m in range(per):
+                mine = slice(m * rows, (m + 1) * rows)
+                part = jnp.where(lane == v_at + m, out[mine], part)
+                here = stat_lane == slot * per + m
+                stat_ref[0] = jnp.where(here, top[mine], stat_ref[0])
+                stat_ref[1] = jnp.where(here, total[mine], stat_ref[1])
+        part_ref[lax.div(base, 2)] = part
+
+    for t in range(n_z):
+        if t == n_z - 1:
+            relay_y(t)
+
+        def chip(u, carry):
+            base = slot_z(t) - core + u * (2 - 4 * y)
+            slot = base + 1 - core
+            put(kv_buf.at[slot], slot, core_sem.at[0], core_peer).wait_recv()
+            attend(base)
+            return carry
+
+        lax.fori_loop(0, 2, chip, 0)
+
+    for t in range(n_z):
+        slot = slot_z(t)
+        if t:
+            put(kv_ref, slot, z_sem.at[t], y_peer).wait_send()
+        put(kv_ref, slot, y_sem.at[t], y_peer).wait_send()
+        for u in range(2):
+            put(kv_ref, slot, core_sem.at[2 * t + u], core_peer).wait_send()
+    for k, peer in enumerate(col_peers):
+        put_q(col, peer, q_send.at[k]).wait_send()
+
+
+def gather_attention(query, key, value, pair, w_bias):
+    n, n_col = lax.axis_size("row"), lax.axis_size("col")
     rows, cols, channels = pair.shape
     heads = w_bias.shape[1]
+    feats = key.shape[1]
+    head_dim = feats * n // heads
+    n_slot = query.shape[1] // feats
     group = 8
     eye = jnp.eye(group, dtype=F32)
     wt = (w_bias.T[:, None, None, :] * eye[None, :, :, None]).reshape(
         heads * group, group * channels
     )
     wt_hi, wt_lo = split(wt)
-    whole = pl.BlockSpec((heads * group, group * channels), lambda i: (0, 0))
+    odd = lax.rem(lax.axis_index("row"), 2) == 1
+    kv = jnp.where(
+        odd, jnp.concatenate([key, value], axis=1), jnp.concatenate([value, key], axis=1)
+    )
+    q = query.reshape(rows, n_slot // 2, 2, feats).transpose(1, 2, 0, 3)
+    zero = jnp.zeros_like(q[:, 0])
+    q = jnp.stack(
+        [jnp.concatenate([zero, q[:, 0]], axis=2), jnp.concatenate([q[:, 1], zero], axis=2)],
+        axis=1,
+    ).reshape(n_slot, rows, 2 * feats)
+    any_space = pl.BlockSpec(memory_space=pl.ANY)
+    vmem = pl.BlockSpec(memory_space=pltpu.VMEM)
+    dma = pltpu.SemaphoreType.DMA
+    n_z = n // 4
     return pl.pallas_call(
-        bias_kernel,
-        out_shape=jax.ShapeDtypeStruct((heads, rows, cols), F32),
-        grid=(rows // group,),
-        in_specs=[pl.BlockSpec((group, cols, channels), lambda i: (i, 0, 0)), whole, whole],
-        out_specs=pl.BlockSpec((heads, group, cols), lambda i: (0, i, 0)),
-        compiler_params=pltpu.CompilerParams(vmem_limit_bytes=VMEM_LIMIT),
-        name="pair_bias",
-    )(pair, wt_hi, wt_lo)
-
-
-def attention_kernel(head_dim, q_ref, k_ref, v_ref, bias_ref, part_ref, top_ref, total_ref):
-    rows = q_ref.shape[0]
-    heads = bias_ref.shape[0]
-    per = 128 // head_dim
-    scale = F32(head_dim) ** -0.5
-    lane = lax.broadcasted_iota(jnp.int32, (rows, 128), 1)
-    tops = jnp.zeros((rows, 128), F32)
-    totals = jnp.zeros((rows, 128), F32)
-    for g in range(heads // per):
-        lanes = slice(g * 128, (g + 1) * 128)
-        q = q_ref[:, lanes]
-        q4 = jnp.concatenate(
-            [jnp.where(lane // head_dim == m, q, 0.0) for m in range(per)], axis=0
-        )
-        bias = bias_ref[g * per : (g + 1) * per].reshape(per * rows, -1)
-        scores = dot_nt(q4, k_ref[:, lanes], HIGH) * scale + bias
-        top = jnp.max(scores, axis=1, keepdims=True)
-        expo = jnp.exp(scores - top)
-        total = jnp.sum(expo, axis=1, keepdims=True)
-        e_hi, e_lo = halves(expo)
-        v_hi, v_lo = halves(v_ref[:, lanes])
-        dot = functools.partial(jnp.dot, preferred_element_type=F32)
-        out = dot(e_hi, v_hi) + (dot(e_hi, v_lo) + dot(e_lo, v_hi))
-        part = jnp.zeros((rows, 128), F32)
-        for m in range(per):
-            mine = slice(m * rows, (m + 1) * rows)
-            part = jnp.where(lane // head_dim == m, out[mine], part)
-            tops = jnp.where(lane == g * per + m, top[mine], tops)
-            totals = jnp.where(lane == g * per + m, total[mine], totals)
-        part_ref[:, lanes] = part
-    top_ref[...] = tops
-    total_ref[...] = totals
-
-
-def attention(q, k, v, bias, head_dim):
-    rows, width = q.shape
-    small = jax.ShapeDtypeStruct((rows, 128), F32)
-    return pl.pallas_call(
-        functools.partial(attention_kernel, head_dim),
-        out_shape=(jax.ShapeDtypeStruct((rows, width), F32), small, small),
-        compiler_params=pltpu.CompilerParams(vmem_limit_bytes=VMEM_LIMIT),
-        name="attention",
-    )(q, k, v, bias)
+        functools.partial(gather_attention_kernel, n, n_col, head_dim, heads),
+        out_shape=(
+            jax.ShapeDtypeStruct((n // 2, rows, 2 * feats), F32),
+            jax.ShapeDtypeStruct((2, rows, 128), F32),
+        ),
+        in_specs=[any_space, any_space, any_space, vmem, vmem],
+        out_specs=(vmem, vmem),
+        scratch_shapes=[
+            pltpu.VMEM((n, cols, 2 * feats), F32),
+            pltpu.VMEM((n, rows, 2 * feats), F32),
+            pltpu.VMEM((heads, rows, cols), F32),
+            pltpu.VMEM((rows // group, group, cols, channels), F32),
+            dma((n,)),
+            dma((n_z,)),
+            dma((n_z,)),
+            dma((2 * n_z,)),
+            dma((n_col,)),
+            dma((n_col,)),
+            dma((rows // group,)),
+        ],
+        compiler_params=pltpu.CompilerParams(
+            vmem_limit_bytes=VMEM_LIMIT, collective_id=0, has_side_effects=True
+        ),
+        name="gather_attention",
+    )(kv, q, pair, wt_hi, wt_lo)
 
 
 def transition_kernel(
@@ -192,11 +334,9 @@
     width = w_out.shape[0]
     head_dim = width // heads
     proj = w_left.shape[1]
-    queries = lax.all_gather(query, "col", axis=1, tiled=True)
-    keys = lax.all_gather(key, "row", axis=1, tiled=True)
-    values = lax.all_gather(value, "row", axis=1, tiled=True)
-    bias = pair_bias(pair, w_bias)
-    part, top, total = attention(queries, keys, values, bias, head_dim)
+    part, stat = gather_attention(query, key, value, pair, w_bias)
+    part = part.transpose(1, 0, 2).reshape(rows, width)
+    top, total = stat[0], stat[1]
     every = lax.all_gather(
         jnp.concatenate([part, top[:, :heads], total[:, :heads]], axis=1), "col"
     )

time: 194 us -> 130 us (0.67)
  waiting for transfers between devices: 58 us -> 0 us
  Pallas kernels: 60.9 us -> 74.9 us
  between operations: 14.2 us -> 0.9 us
  local copies, waits for them, and re-layouts: 14.2 us -> 9.66 us
  blocking collectives: 39.9 us -> 36.7 us
    all_gather x2 -> x0, waiting for transfers between devices: 56.6 us -> none  [the longest x1 37.6 us: per_device(): values = lax.all_gather(value, 'row', axis=1, tiled=True)]
    pallas_call x2 -> x1, Pallas kernels: 21.2 us -> 35.1 us  [gather_attention(): pl.pallas_call(functools.partial(gather_attention_kernel, n, n_col, head_...]
    all_gather x1 -> x0, blocking collectives: 6.51 us -> none  [per_device(): queries = lax.all_gather(query, 'col', axis=1, tiled=True)]
    all_gather x2 -> x0, local copies, waits for them, and re-layouts: 6.04 us -> none  [the longest x1 3.02 us: per_device(): values = lax.all_gather(value, 'row', axis=1, tiled=True)]
    all_gather x1, blocking collectives: 20.2 us -> 23.5 us  [per_device(): right_every = lax.all_gather(both[:, proj:], 'row', axis=0, tiled=True)]
    reshape x0 -> x3, local copies, waits for them, and re-layouts: none -> 2.18 us  [the longest x2 1.24 us: gather_attention(): q = query.reshape(rows, n_slot // 2, 2, feats).transpose(1, 2, 0, 3)]
  transfers between devices with their start and end apart: 2 -> 0, of which waited for: 2 -> 0; matrix products, arithmetic and copies ran while one was open for 4% -> 0% of each run, Pallas kernels for 7% -> 0%
where the time goes in v2:
time: 130 us; the launch traced here: 129 us
  Pallas kernels  74.9 us (58%)
  blocking collectives  36.7 us (28%)
  local copies, waits for them, and re-layouts  9.66 us (7%)
  other arithmetic  5.29 us (4%)
  matrix products  1.87 us (1%)
    pallas_call x1, Pallas kernels, transition(): pl.pallas_call(transition_kernel, out_shape=jax.ShapeDtypeStruct(pair.sha...  39.8 us
    pallas_call x1, Pallas kernels, gather_attention(): pl.pallas_call(functools.partial(gather_attention_kernel, n, n_col, head_...  35.1 us
    all_gather x1, blocking collectives, per_device(): right_every = lax.all_gather(both[:, proj:], 'row', axis=0, tiled=True)  23.5 us
    all_gather x1, blocking collectives, per_device(): lax.all_gather(jnp.concatenate([part, top[:, :heads], total[:, :heads]],...  8.22 us
    all_gather x1, blocking collectives, per_device(): every = lax.all_gather(sent, 'col')  5.01 us

profile of v2, /device:TPU:0, one launch (start us, length us, event | category | flops | bytes accessed | tf_op | source)
XLA Modules:
  0.0 129.3 jit_solution(7778284574715468163)
XLA Ops:
  0.6 0.0 copy-start
  0.6 0.0 copy-start.3
  0.7 0.0 copy-start.6
  0.7 0.0 copy-start.5
  0.7 0.0 copy-start.8
  0.7 1.2 reshape.70
  2.0 0.0 copy-start.4
  2.0 0.1 pad_bitcast_fusion
  2.1 0.7 pad_maximum_fusion.2
  2.8 0.0 copy-start.9
  2.8 1.0 copy.24
  3.8 0.0 copy-done.8
  3.8 0.1 copy.25
  4.0 0.9 maximum_select_fusion.kv_ref
  4.8 0.0 copy-done.5
  4.8 0.0 copy-done.6
  4.9 0.1 reduce_sum.84
  5.0 0.0 copy-done.3
  5.0 0.8 pad_maximum_fusion.up_ref
  5.8 0.0 copy-done.4
  5.9 0.0 copy-start.1
  5.9 0.7 pad_maximum_fusion.1.down_ref
  6.6 0.0 copy-done.9
  6.6 1.2 fusion
  7.9 35.1 %gather_attention.1 = (f32[8,48,128]{2,1,0:T(8,128)}, f32[2,48,128]{2,1,0:T(8,128)}) custom-call(f32[384,128]{1,0:T(8,128)} %maximum_select_fusion.kv_ref, f32[8,48,128]{2,1,0:T(8,128)} %bitcast.50, f32[48,384,128]{2,1,0:T(8,128)} %pair_ref.3, bf16[256,1024]{1,0:T(8,128)(2,1)} %get-tuple-element.20.wt_hi_ref, bf16[256,1024]{1,0:T(8,128)(2,1)} %get-tuple-element.19.wt_lo_ref), custom_call_target="tpu_custom_call" | custom-call | tf_op jit(solution)/shard_map/gather_attention/pallas_call | solution.py:228
  43.0 0.0 copy-done.1
  43.0 0.9 copy_bitcast_fusion
  43.9 0.8 slice_bitcast_fusion.2
  44.7 0.1 concatenate.31
  44.8 8.2 %all-gather = f32[96,1088]{1,0:T(8,128)S(1)} all-gather(f32[48,1088]{1,0:T(8,128)S(1)} %concatenate.31), channel_id=2, replica_groups=mesh['row'=16,'col'=2] {'col'}, dimensions={0}, use_global_device_ids=true | all-gather | bytes 626688 | tf_op jit(solution)/shard_map/all_gather | solution.py:340
  53.0 0.1 fusion.8
  53.1 0.0 copy-start.7
  53.1 1.6 %broadcast_in_dim.6 = f32[2,48,32,32]{3,2,1,0:T(8,128)} broadcast(f32[2,48,32]{2,1,0:T(8,128)S(1)} %fusion.10), dimensions={0,1,2} | broadcast | bytes 405504 | tf_op jit(solution)/shard_map/broadcast_in_dim | solution.py:348
  54.7 2.1 %reshape.73 = f32[2,48,1024]{2,1,0:T(8,128)S(1)} reshape(f32[2,48,32,32]{3,2,1,0:T(8,128)} %broadcast_in_dim.6) | data formatting | bytes 786432 | tf_op jit(solution)/shard_map/reshape | solution.py:348
  56.9 0.0 copy-done
  56.9 0.0 copy-done.7
  56.9 1.4 %fusion.14 = (f32[48]{0:T(128)S(1)}, f32[48,512]{1,0:T(8,128)S(1)}) fusion(f32[48,512]{1,0:T(8,128)S(1)} %copy-done.7, f32[48,1024]{1,0:T(8,128)S(1)} %fusion.1, f32[1024,512]{1,0:T(8,128)S(1)} %copy-done), kind=kOutput, calls=%fused_computation.52 | convolution fusion | flops 302038976 | bytes 2490560 | tf_op jit(solution)/shard_map/dot_general | solution.py:349
  58.4 0.0 copy-start.2
  58.4 0.4 fusion.4
  58.8 0.2 multiply_reduce_fusion
  59.0 0.1 copy.32
  59.1 0.1 copy.31
  59.2 0.1 pad_maximum_fusion.3
  59.3 5.0 %all-gather.1 = f32[96,258]{1,0:T(8,128)S(1)} all-gather(f32[48,258]{1,0:T(8,128)S(1)} %pad_maximum_fusion.3), channel_id=3, replica_groups=mesh['row'=16,'col'=2] {'col'}, dimensions={0}, use_global_device_ids=true | all-gather | bytes 148608 | tf_op jit(solution)/shard_map/all_gather | solution.py:358
  64.3 0.2 slice_reduce_fusion
  64.5 0.1 copy.34
  64.6 0.1 fusion.7
  64.7 0.1 broadcast_multiply_fusion
  64.8 0.6 fusion.13
  65.4 23.5 %all_gather.19 = f32[768,64]{1,0:T(8,128)S(1)} all-gather(f32[48,64]{1,0:T(8,128)S(1)} %get-tuple-element.17), channel_id=1, replica_groups=mesh['row'=16,'col'=2] {'row'}, dimensions={0}, use_global_device_ids=true | all-gather | bytes 208896 | tf_op jit(solution)/shard_map/all_gather | solution.py:367
  88.8 0.7 constant_dynamic-slice_fusion.right_ref
  89.5 39.8 %transition.1 = f32[48,384,128]{2,1,0:T(8,128)} custom-call(f32[48,384,128]{2,1,0:T(8,128)} %pair_ref.3, f32[48,64]{1,0:T(8,128)} %get-tuple-element.18.left_ref, f32[384,64]{1,0:T(8,128)} %constant_dynamic-slice_fusion.right_ref, f32[128,128]{1,0:T(8,128)} %w_outer_ref.1, f32[1,128]{1,0:T(1,128)} %bitcast.55, bf16[384,512]{1,0:T(8,128)(2,1)} %pad_maximum_fusion.up_ref, ...), custom_call_target="tpu_custom_call" | custom-call | tf_op jit(solution)/shard_map/transition/pallas_call | solution.py:313
  129.3 0.0 copy-done.2
  (15 shorter events, 0.3 us)
Async XLA Ops:
  0.6 56.3 %copy-start = (f32[1024,512]{1,0:T(8,128)S(1)}, f32[1024,512]{1,0:T(8,128)}, u32[]{:S(2)}) copy-start(f32[1024,512]{1,0:T(8,128)} %param.19) | copy-start | bytes 6291460
  0.6 4.3 %copy-start.3 = (f32[128,512]{1,0:T(8,128)S(1)}, f32[128,512]{1,0:T(8,128)}, u32[]{:S(2)}) copy-start(f32[128,512]{1,0:T(8,128)} %param.24) | copy-start | bytes 786436
  0.7 4.2 %copy-start.6 = (f32[512,64]{0,1:T(8,128)S(1)}, f32[512,64]{0,1:T(8,128)}, u32[]{:S(2)}) copy-start(f32[512,64]{0,1:T(8,128)} %param.21) | copy-start | bytes 393220
  0.7 4.2 %copy-start.5 = (f32[512,64]{0,1:T(8,128)S(1)}, f32[512,64]{0,1:T(8,128)}, u32[]{:S(2)}) copy-start(f32[512,64]{0,1:T(8,128)} %param.20) | copy-start | bytes 393220
  0.7 3.2 %copy-start.8 = (f32[384,64]{0,1:T(8,128)S(1)}, f32[384,64]{0,1:T(8,128)}, u32[]{:S(2)}) copy-start(f32[384,64]{0,1:T(8,128)} %param.16) | copy-start | bytes 294916
  2.0 3.9 %copy-start.4 = (f32[512,128]{1,0:T(8,128)S(1)}, f32[512,128]{1,0:T(8,128)}, u32[]{:S(2)}) copy-start(f32[512,128]{1,0:T(8,128)} %param.25) | copy-start | bytes 786436
  2.8 3.8 %copy-start.9 = (f32[128,32]{0,1:T(8,128)S(1)}, f32[128,32]{0,1:T(8,128)}, u32[]{:S(2)}) copy-start(f32[128,32]{0,1:T(8,128)} %param.18) | copy-start | bytes 49156
  5.9 37.1 %copy-start.1 = (bf16[512,128]{1,0:T(8,128)(2,1)}, bf16[512,128]{1,0:T(8,128)(2,1)S(1)}, u32[]{:S(2)}) copy-start(bf16[512,128]{1,0:T(8,128)(2,1)S(1)} %get-tuple-element.8.down_hi_ref) | copy-start | bytes 393220
  53.1 3.8 %copy-start.7 = (f32[48,512]{1,0:T(8,128)S(1)}, f32[48,512]{1,0:T(8,128)}, u32[]{:S(2)}) copy-start(f32[48,512]{1,0:T(8,128)} %param.13) | copy-start | bytes 294916
  58.4 70.9 %copy-start.2 = (f32[48,512]{1,0:T(8,128)}, f32[48,512]{1,0:T(8,128)S(1)}, u32[]{:S(2)}) copy-start(f32[48,512]{1,0:T(8,128)S(1)} %get-tuple-element.26) | copy-start | bytes 294916

commit v3 on v2

--- a/solution.py
+++ b/solution.py
@@ -253,6 +253,183 @@
     )(kv, q, pair, wt_hi, wt_lo)
 
 
+def merge_kernel(
+    n, n_col, head_dim, heads,
+    part_ref, stat_ref, seq_ref, w_out_ref, w_both_ref,
+    seq_out, left_out, right_out,
+    part_buf, stat_buf, packet, packet_buf, both_buf, right_buf,
+    part_send, part_recv, stat_send, stat_recv, pack_send, pack_recv,
+    right_send, right_recv, relay_send,
+):
+    rows, here = seq_ref.shape
+    width = w_out_ref.shape[0]
+    proj = left_out.shape[1]
+    blocks = right_buf.shape[0]
+    row, col = lax.axis_index("row"), lax.axis_index("col")
+    core = lax.rem(row, 2)
+    core_peer = row + 1 - 2 * core
+    col_peers = [lax.rem(col + k, n_col) for k in range(1, n_col)]
+    row_peers = [lax.rem(row + 2 * k, n) for k in range(1, n // 2)]
+
+    barrier = pltpu.get_barrier_semaphore()
+    for peer in row_peers + [core_peer]:
+        pl.semaphore_signal(barrier, inc=1, device_id={"row": peer}, device_id_type=MESH)
+    for peer in col_peers:
+        pl.semaphore_signal(barrier, inc=1, device_id={"col": peer}, device_id_type=MESH)
+    pl.semaphore_wait(barrier, n // 2 + n_col - 1)
+
+    def put(src, dst, send, recv, peer):
+        return pltpu.make_async_remote_copy(
+            src_ref=src, dst_ref=dst, send_sem=send, recv_sem=recv,
+            device_id=peer, device_id_type=MESH,
+        )
+
+    def over_col(src, buf, send, recv):
+        return [
+            put(src, buf.at[k], send.at[k], recv.at[k], {"col": peer})
+            for k, peer in enumerate(col_peers)
+        ]
+
+    stats = over_col(stat_ref, stat_buf, stat_send, stat_recv)
+    parts = over_col(part_ref, part_buf, part_send, part_recv)
+    for copy in stats + parts:
+        copy.start()
+    for copy in stats:
+        copy.wait()
+    tops = [stat_ref[0]] + [stat_buf[k, 0] for k in range(n_col - 1)]
+    totals = [stat_ref[1]] + [stat_buf[k, 1] for k in range(n_col - 1)]
+    highest = functools.reduce(jnp.maximum, tops)
+    scales = [jnp.exp(top - highest) for top in tops]
+    total = sum(scale * t for scale, t in zip(scales, totals))
+    lane = lax.broadcasted_iota(jnp.int32, total.shape, 1)
+    total = jnp.where(lane < heads, total, 1.0)
+    spread_of = (
+        lax.broadcasted_iota(jnp.int32, (total.shape[1], width), 0)
+        == lax.broadcasted_iota(jnp.int32, (total.shape[1], width), 1) // head_dim
+    ).astype(F32)
+    weights = [
+        jnp.dot(scale / total, spread_of, precision=HIGH, preferred_element_type=F32)
+        for scale in scales
+    ]
+    for copy in parts:
+        copy.wait()
+
+    def dense(load):
+        return jnp.concatenate([load(m) for m in range(part_ref.shape[0])], axis=1)
+
+    attn = dense(lambda m: part_ref[m]) * weights[0]
+    for k in range(n_col - 1):
+        attn = attn + dense(lambda m: part_buf[k, m]) * weights[k + 1]
+    seq_new = seq_ref[...] + jnp.dot(
+        attn, w_out_ref[...], precision=HIGH, preferred_element_type=F32
+    )
+    seq_out[...] = seq_new
+
+    local_mean = jnp.mean(seq_new, axis=1, keepdims=True)
+    centred = seq_new - local_mean
+    spread = jnp.sum(centred * centred, axis=1, keepdims=True)
+    w_both = w_both_ref[...]
+    packet[:rows] = jnp.dot(centred, w_both, precision=HIGH, preferred_element_type=F32)
+    lane = lax.broadcasted_iota(jnp.int32, (rows, 2 * proj), 1)
+    packet[rows : 2 * rows] = jnp.where(lane < proj, local_mean, spread)
+    packet[2 * rows :] = jnp.broadcast_to(
+        jnp.sum(w_both, axis=0, keepdims=True), (8, 2 * proj)
+    )
+    packets = over_col(packet, packet_buf, pack_send, pack_recv)
+    for copy in packets:
+        copy.start()
+    for copy in packets:
+        copy.wait()
+    every = [packet[...]] + [packet_buf[k] for k in range(n_col - 1)]
+    means = [p[rows : 2 * rows, :1] for p in every]
+    mean = sum(means) / n_col
+    offsets = [m - mean for m in means]
+    variance = (
+        sum(p[rows : 2 * rows, proj : proj + 1] for p in every)
+        + here * sum(o * o for o in offsets)
+    ) / width
+    both = sum(p[:rows] + o * p[2 * rows : 2 * rows + 1] for p, o in zip(every, offsets))
+    both = both * lax.rsqrt(variance + 1e-05)
+    left_out[...] = both[:, :proj]
+    both_buf[...] = both
+
+    mine = lax.div(row, blocks) == col
+    own = lax.rem(row, blocks)
+
+    def row_copies():
+        return [
+            put(both_buf, right_buf.at[own], right_send.at[k], right_recv.at[own], {"row": peer})
+            for k, peer in enumerate(row_peers)
+        ]
+
+    @pl.when(mine)
+    def _():
+        for copy in row_copies():
+            copy.start()
+        keep = pltpu.make_async_copy(both_buf, right_buf.at[own], right_recv.at[own])
+        keep.start()
+        keep.wait()
+
+    def relay(j, block):
+        slot = right_buf.at[block]
+        return put(slot, slot, relay_send.at[j], right_recv.at[block], {"row": core_peer})
+
+    for j in range(blocks // 2):
+        block = 2 * j + core
+
+        @pl.when(col * blocks + block != row)
+        def _():
+            relay(j, block).wait_recv()
+
+        relay(j, block).start()
+    for j in range(blocks // 2):
+        relay(j, 2 * j + 1 - core).wait_recv()
+    for b in range(blocks):
+        right_out[b * rows : (b + 1) * rows] = right_buf[b][:, proj:]
+    for j in range(blocks // 2):
+        relay(j, 2 * j + core).wait_send()
+
+    @pl.when(mine)
+    def _():
+        for copy in row_copies():
+            copy.wait_send()
+
+
+def merge(part, stat, seq, w_out, w_left, w_right, head_dim, heads, cols):
+    n, n_col = lax.axis_size("row"), lax.axis_size("col")
+    rows = seq.shape[0]
+    proj = w_left.shape[1]
+    blocks = cols // rows
+    w_both = jnp.concatenate([w_left, w_right], axis=1)
+    vmem = pl.BlockSpec(memory_space=pltpu.VMEM)
+    dma = pltpu.SemaphoreType.DMA
+    peers = n_col - 1
+    return pl.pallas_call(
+        functools.partial(merge_kernel, n, n_col, head_dim, heads),
+        out_shape=(
+            jax.ShapeDtypeStruct(seq.shape, F32),
+            jax.ShapeDtypeStruct((rows, proj), F32),
+            jax.ShapeDtypeStruct((cols, proj), F32),
+        ),
+        in_specs=[vmem] * 5,
+        out_specs=(vmem,) * 3,
+        scratch_shapes=[
+            pltpu.VMEM((peers, *part.shape), F32),
+            pltpu.VMEM((peers, *stat.shape), F32),
+            pltpu.VMEM((2 * rows + 8, 2 * proj), F32),
+            pltpu.VMEM((peers, 2 * rows + 8, 2 * proj), F32),
+            pltpu.VMEM((rows, 2 * proj), F32),
+            pltpu.VMEM((blocks, rows, 2 * proj), F32),
+            dma((peers,)), dma((peers,)), dma((peers,)), dma((peers,)), dma((peers,)),
+            dma((peers,)), dma((n // 2 - 1,)), dma((blocks,)), dma((blocks // 2,)),
+        ],
+        compiler_params=pltpu.CompilerParams(
+            vmem_limit_bytes=VMEM_LIMIT, collective_id=1, has_side_effects=True
+        ),
+        name="merge",
+    )(part, stat, seq, w_out, w_both)
+
+
 def transition_kernel(
     pair_ref, left_ref, right_ref, w_outer_ref, bias_ref, up_ref, down_ref, down_hi_ref, out_ref,
     left_t, right_s, left_d,
@@ -333,39 +510,10 @@
     heads = w_bias.shape[1]
     width = w_out.shape[0]
     head_dim = width // heads
-    proj = w_left.shape[1]
     part, stat = gather_attention(query, key, value, pair, w_bias)
-    part = part.transpose(1, 0, 2).reshape(rows, width)
-    top, total = stat[0], stat[1]
-    every = lax.all_gather(
-        jnp.concatenate([part, top[:, :heads], total[:, :heads]], axis=1), "col"
-    )
-    parts = every[:, :, :width]
-    tops = every[:, :, width : width + heads]
-    totals = every[:, :, width + heads :]
-    scale = jnp.exp(tops - jnp.max(tops, axis=0))
-    scale = scale / jnp.sum(scale * totals, axis=0)
-    attn = jnp.sum(parts * jnp.repeat(scale, head_dim, axis=2), axis=0)
-    seq_new = seq + jnp.dot(attn, w_out, precision=HIGH)
-    here = seq.shape[1]
-    local_mean = jnp.mean(seq_new, axis=1, keepdims=True)
-    centred = seq_new - local_mean
-    w_both = jnp.concatenate([w_left, w_right], axis=1)
-    projected = jnp.dot(centred, w_both, precision=HIGH)
-    spread = jnp.sum(centred * centred, axis=1, keepdims=True)
-    column = jnp.broadcast_to(jnp.sum(w_both, axis=0, keepdims=True), (rows, 2 * proj))
-    sent = jnp.concatenate([projected, column, local_mean, spread], axis=1)
-    every = lax.all_gather(sent, "col")
-    means = every[:, :, 4 * proj : 4 * proj + 1]
-    spreads = every[:, :, 4 * proj + 1 :]
-    mean = jnp.mean(means, axis=0)
-    offset = means - mean
-    variance = (jnp.sum(spreads, axis=0) + here * jnp.sum(offset * offset, axis=0)) / width
-    both = jnp.sum(every[:, :, : 2 * proj] + offset * every[:, :, 2 * proj : 4 * proj], axis=0)
-    both = both * lax.rsqrt(variance + 1e-05)
-    left = both[:, :proj]
-    right_every = lax.all_gather(both[:, proj:], "row", axis=0, tiled=True)
-    right = lax.dynamic_slice_in_dim(right_every, lax.axis_index("col") * cols, cols, 0)
+    seq_new, left, right = merge(
+        part, stat, seq, w_out, w_left, w_right, head_dim, heads, cols
+    )
     pair_new = transition(pair, left, right, w_outer, outer_bias, w_up, w_down)
     return seq_new, pair_new
 

time: 130 us -> 116 us (0.89)
  blocking collectives: 36.7 us -> 0 us
  Pallas kernels: 74.9 us -> 101 us
  local copies, waits for them, and re-layouts: 9.66 us -> 5.94 us
  other arithmetic: 5.29 us -> 7.88 us
  matrix products: 1.87 us -> 0 us
    all_gather x3 -> x0, blocking collectives: 36.7 us -> none  [the longest x1 23.5 us: per_device(): right_every = lax.all_gather(both[:, proj:], 'row', axis=0, tiled=True)]
    pallas_call x0 -> x1, Pallas kernels: none -> 26.2 us  [merge(): pl.pallas_call(functools.partial(merge_kernel, n, n_col, head_dim, heads)...]
    unnamed x24 -> x9, local copies, waits for them, and re-layouts: 1.29 us -> 4.74 us
    reshape x2 -> x0, local copies, waits for them, and re-layouts: 3.06 us -> none  [the longest x1 2.12 us: per_device(): attn = jnp.sum(parts * jnp.repeat(scale, head_dim, axis=2), axis=0)]
    convert_element_type x3, other arithmetic: 1.31 us -> 3.92 us  [split(): return (kept.astype(BF16), (x - kept).astype(BF16))]
    dot_general x2 -> x0, matrix products: 1.87 us -> none  [the longest x1 1.45 us: per_device(): seq_new = seq + jnp.dot(attn, w_out, precision=HIGH)]
    broadcast_in_dim x2 -> x0, local copies, waits for them, and re-layouts: 1.71 us -> none  [the longest x1 1.61 us: per_device(): attn = jnp.sum(parts * jnp.repeat(scale, head_dim, axis=2), axis=0)]
where the time goes in v3:
time: 116 us
  Pallas kernels  101 us (87%)
  other arithmetic  7.88 us (7%)
  local copies, waits for them, and re-layouts  5.94 us (5%)
    pallas_call x1, Pallas kernels, transition(): pl.pallas_call(transition_kernel, out_shape=jax.ShapeDtypeStruct(pair.sha...  39.8 us
    pallas_call x1, Pallas kernels, gather_attention(): pl.pallas_call(functools.partial(gather_attention_kernel, n, n_col, head_...  35.1 us
    pallas_call x1, Pallas kernels, merge(): pl.pallas_call(functools.partial(merge_kernel, n, n_col, head_dim, heads)...  26.2 us
    unnamed x9, local copies, waits for them, and re-layouts  4.74 us
    convert_element_type x3, other arithmetic, split(): return (kept.astype(BF16), (x - kept).astype(BF16))  3.92 us

profile of v3, /device:TPU:0, one launch (start us, length us, event | category | flops | bytes accessed | tf_op | source)
XLA Modules:
  0.0 115.6 jit_solution(17791975188146125795)
XLA Ops:
  0.6 1.0 reshape.26
  1.8 0.1 pad_bitcast_fusion
  1.9 0.7 pad_maximum_fusion.3
  2.6 1.0 copy.15
  3.6 1.0 copy.16
  4.6 0.9 maximum_select_fusion.kv_ref
  5.5 1.0 copy.21
  6.5 1.0 copy.22
  7.5 0.9 pad_maximum_fusion.1.w_both_ref
  8.4 1.0 reduce-precision_convert_fusion.2
  9.4 0.8 pad_maximum_fusion.up_ref
  10.2 1.0 reduce-precision_convert_fusion.1
  11.2 0.0 copy-start
  11.2 0.7 pad_maximum_fusion.2.down_ref
  11.9 1.9 %fusion = (bf16[256,1024]{1,0:T(8,128)(2,1)}, bf16[256,1024]{1,0:T(8,128)(2,1)}) fusion(f32[8,8]{0,1:T(8,128)S(1)} %fusion.3, f32[32,128]{1,0:T(8,128)} %bitcast.21), kind=kLoop, calls=%fused_computation.2 | loop fusion | flops 1310720 | bytes 1065216 | tf_op jit(solution)/shard_map/convert_element_type | solution.py:25
  13.9 35.1 %gather_attention.1 = (f32[8,48,128]{2,1,0:T(8,128)}, f32[2,48,128]{2,1,0:T(8,128)}) custom-call(f32[384,128]{1,0:T(8,128)} %maximum_select_fusion.kv_ref, f32[8,48,128]{2,1,0:T(8,128)} %bitcast.20, f32[48,384,128]{2,1,0:T(8,128)} %pair_ref.3, bf16[256,1024]{1,0:T(8,128)(2,1)} %get-tuple-element.19.wt_hi_ref, bf16[256,1024]{1,0:T(8,128)(2,1)} %get-tuple-element.18.wt_lo_ref), custom_call_target="tpu_custom_call" | custom-call | tf_op jit(solution)/shard_map/gather_attention/pallas_call | solution.py:228
  49.0 26.2 %merge.1 = (f32[48,512]{1,0:T(8,128)}, f32[48,64]{1,0:T(8,128)}, f32[384,64]{1,0:T(8,128)}) custom-call(f32[8,48,128]{2,1,0:T(8,128)} %get-tuple-element.7.part_ref, f32[2,48,128]{2,1,0:T(8,128)} %get-tuple-element.8.stat_ref, f32[48,512]{1,0:T(8,128)} %seq_ref.1, f32[1024,512]{1,0:T(8,128)} %w_out_ref.1, f32[512,128]{1,0:T(8,128)} %pad_maximum_fusion.1.w_both_ref), custom_call_target="tpu_custom_call" | custom-call | tf_op jit(solution)/shard_map/merge/pallas_call | solution.py:407
  75.2 0.0 copy-done
  75.2 0.0 copy-start.1
  75.2 39.8 %transition.1 = f32[48,384,128]{2,1,0:T(8,128)} custom-call(f32[48,384,128]{2,1,0:T(8,128)} %pair_ref.3, f32[48,64]{1,0:T(8,128)} %get-tuple-element.10.left_ref, f32[384,64]{1,0:T(8,128)} %get-tuple-element.11.right_ref, f32[128,128]{1,0:T(8,128)} %w_outer_ref.1, f32[1,128]{1,0:T(1,128)} %bitcast.22, bf16[384,512]{1,0:T(8,128)(2,1)} %pad_maximum_fusion.up_ref, ...), custom_call_target="tpu_custom_call" | custom-call | tf_op jit(solution)/shard_map/transition/pallas_call | solution.py:490
  115.0 0.0 copy-done.1
  115.0 0.6 copy.26
  (3 shorter events, 0.1 us)
Async XLA Ops:
  11.2 64.0 %copy-start = (bf16[512,128]{1,0:T(8,128)(2,1)}, bf16[512,128]{1,0:T(8,128)(2,1)S(1)}, u32[]{:S(2)}) copy-start(bf16[512,128]{1,0:T(8,128)(2,1)S(1)} %get-tuple-element.12.down_hi_ref) | copy-start | bytes 393220
  75.2 39.8 %copy-start.1 = (f32[48,512]{1,0:T(8,128)S(1)}, f32[48,512]{1,0:T(8,128)}, u32[]{:S(2)}) copy-start(f32[48,512]{1,0:T(8,128)} %get-tuple-element.24) | copy-start | bytes 294916

commit v4 on v3

--- a/solution.py
+++ b/solution.py
@@ -431,8 +431,8 @@
 
 
 def transition_kernel(
-    pair_ref, left_ref, right_ref, w_outer_ref, bias_ref, up_ref, down_ref, down_hi_ref, out_ref,
-    left_t, right_s, left_d,
+    pair_ref, left_ref, right_ref, w_outer_ref, bias_ref, w_up_ref, w_down_ref, out_ref,
+    left_t, right_s, left_d, up_ref, down_ref, down_hi_ref,
 ):
     step = pl.program_id(0)
     group, cols, channels = pair_ref.shape
@@ -446,6 +446,11 @@
         left_d[...] = jnp.dot(left, w_outer_ref[proj:], precision=HIGH) + bias_ref[...]
         r_hi, r_lo = halves(right_ref[...])
         right_s[...] = jnp.concatenate([r_hi, r_lo, r_hi], axis=1)
+        up_hi, up_lo = halves(w_up_ref[...])
+        up_ref[...] = jnp.concatenate([up_hi, up_hi, up_lo], axis=0)
+        down_hi, down_lo = halves(w_down_ref[...])
+        down_ref[...] = jnp.concatenate([down_hi, down_lo], axis=1)
+        down_hi_ref[...] = down_hi
 
     lane = lax.broadcasted_iota(jnp.int32, left_t.shape, 1)
     w_prod = w_outer_ref[:proj]
@@ -476,17 +481,13 @@
     rows, cols, channels = pair.shape
     proj = left.shape[1]
     hidden = w_up.shape[1]
-    group = 2
-    up_hi, up_lo = split(w_up)
-    up = jnp.concatenate([up_hi, up_hi, up_lo], axis=0)
-    down_hi, down_lo = split(w_down)
-    down = jnp.concatenate([down_hi, down_lo], axis=1)
+    group = 4
 
     def whole(x):
         return pl.BlockSpec(x.shape, lambda i: (0,) * x.ndim)
 
     block = pl.BlockSpec((group, cols, channels), lambda i: (i, 0, 0))
-    fixed = (left, right, w_outer, outer_bias.reshape(1, channels), up, down, down_hi)
+    fixed = (left, right, w_outer, outer_bias.reshape(1, channels), w_up, w_down)
     return pl.pallas_call(
         transition_kernel,
         out_shape=jax.ShapeDtypeStruct(pair.shape, F32),
@@ -497,6 +498,9 @@
             pltpu.VMEM((proj, rows), F32),
             pltpu.VMEM((cols, 3 * proj), BF16),
             pltpu.VMEM((rows, channels), F32),
+            pltpu.VMEM((3 * channels, hidden), BF16),
+            pltpu.VMEM((hidden, 2 * channels), BF16),
+            pltpu.VMEM((hidden, channels), BF16),
         ],
         compiler_params=pltpu.CompilerParams(vmem_limit_bytes=VMEM_LIMIT),
         name="transition",

time: 116 us -> 105 us (0.905)
  Pallas kernels: 101 us -> 93.2 us
  other arithmetic: 7.88 us -> 4.35 us
    pallas_call x1, Pallas kernels: 39.8 us -> 31.9 us  [transition(): pl.pallas_call(transition_kernel, out_shape=jax.ShapeDtypeStruct(pair.sha...]
    convert_element_type x3 -> x1, other arithmetic: 3.92 us -> 1.95 us  [split(): return (kept.astype(BF16), (x - kept).astype(BF16))]
    concatenate x2 -> x0, other arithmetic: 1.53 us -> none  [the longest x1 0.78 us: transition(): up = jnp.concatenate([up_hi, up_hi, up_lo], axis=0)]
    unnamed x9 -> x7, local copies, waits for them, and re-layouts: 4.74 us -> 4.74 us
where the time goes in v4:
time: 105 us; the launch traced here: 104 us
  Pallas kernels  93.2 us (89%)
  local copies, waits for them, and re-layouts  5.94 us (6%)
  other arithmetic  4.35 us (4%)
    pallas_call x1, Pallas kernels, gather_attention(): pl.pallas_call(functools.partial(gather_attention_kernel, n, n_col, head_...  35.1 us
    pallas_call x1, Pallas kernels, transition(): pl.pallas_call(transition_kernel, out_shape=jax.ShapeDtypeStruct(pair.sha...  31.9 us
    pallas_call x1, Pallas kernels, merge(): pl.pallas_call(functools.partial(merge_kernel, n, n_col, head_dim, heads)...  26.2 us
    unnamed x7, local copies, waits for them, and re-layouts  4.74 us

profile of v4, /device:TPU:0, one launch (start us, length us, event | category | flops | bytes accessed | tf_op | source)
XLA Modules:
  0.0 104.2 jit_solution(15495554719512928892)
XLA Ops:
  0.6 1.0 %reshape.26 = f32[48,4,2,64]{3,2,1,0:T(2,128)S(1)} reshape(f32[48,512]{1,0:T(8,128)} %param.14) | data formatting | bytes 196608 | tf_op jit(solution)/shard_map/reshape | solution.py:218
  1.8 0.1 pad_bitcast_fusion
  1.9 0.7 pad_maximum_fusion.1
  2.6 1.0 copy.15
  3.6 1.0 copy.16
  4.6 0.9 maximum_select_fusion.kv_ref
  5.5 1.0 copy.21
  6.5 1.0 copy.22
  7.5 0.8 pad_maximum_fusion.w_both_ref
  8.4 1.9 %fusion = (bf16[256,1024]{1,0:T(8,128)(2,1)}, bf16[256,1024]{1,0:T(8,128)(2,1)}) fusion(f32[8,8]{0,1:T(8,128)S(1)} %fusion.1, f32[32,128]{1,0:T(8,128)} %bitcast.21), kind=kLoop, calls=%fused_computation.2 | loop fusion | flops 1310720 | bytes 1065216 | tf_op jit(solution)/shard_map/convert_element_type | solution.py:25
  10.3 35.1 %gather_attention.1 = (f32[8,48,128]{2,1,0:T(8,128)}, f32[2,48,128]{2,1,0:T(8,128)}) custom-call(f32[384,128]{1,0:T(8,128)} %maximum_select_fusion.kv_ref, f32[8,48,128]{2,1,0:T(8,128)} %bitcast.20, f32[48,384,128]{2,1,0:T(8,128)} %pair_ref.3, bf16[256,1024]{1,0:T(8,128)(2,1)} %get-tuple-element.15.wt_hi_ref, bf16[256,1024]{1,0:T(8,128)(2,1)} %get-tuple-element.14.wt_lo_ref), custom_call_target="tpu_custom_call" | custom-call | tf_op jit(solution)/shard_map/gather_attention/pallas_call | solution.py:228
  45.4 26.2 %merge.1 = (f32[48,512]{1,0:T(8,128)}, f32[48,64]{1,0:T(8,128)}, f32[384,64]{1,0:T(8,128)}) custom-call(f32[8,48,128]{2,1,0:T(8,128)} %get-tuple-element.7.part_ref, f32[2,48,128]{2,1,0:T(8,128)} %get-tuple-element.8.stat_ref, f32[48,512]{1,0:T(8,128)} %seq_ref.1, f32[1024,512]{1,0:T(8,128)} %w_out_ref.1, f32[512,128]{1,0:T(8,128)} %pad_maximum_fusion.w_both_ref), custom_call_target="tpu_custom_call" | custom-call | tf_op jit(solution)/shard_map/merge/pallas_call | solution.py:407
  71.6 0.0 copy-start
  71.6 31.9 %transition.1 = f32[48,384,128]{2,1,0:T(8,128)} custom-call(f32[48,384,128]{2,1,0:T(8,128)} %pair_ref.3, f32[48,64]{1,0:T(8,128)} %get-tuple-element.10.left_ref, f32[384,64]{1,0:T(8,128)} %get-tuple-element.11.right_ref, f32[128,128]{1,0:T(8,128)} %w_outer_ref.1, f32[1,128]{1,0:T(1,128)} %bitcast.22, f32[128,512]{1,0:T(8,128)} %w_up_ref.1, ...), custom_call_target="tpu_custom_call" | custom-call | tf_op jit(solution)/shard_map/transition/pallas_call | solution.py:491
  103.5 0.0 copy-done
  103.5 0.6 copy.26
  (3 shorter events, 0.1 us)
Async XLA Ops:
  71.6 31.9 %copy-start = (f32[48,512]{1,0:T(8,128)S(1)}, f32[48,512]{1,0:T(8,128)}, u32[]{:S(2)}) copy-start(f32[48,512]{1,0:T(8,128)} %get-tuple-element.20) | copy-start | bytes 294916
